TPU v7x, 128 devices: a whole 4x4x4 slice. The times are simulated.
128 devices in a mesh: segment: 2 (over z_hi), win: 16 (over y, z_lo, core), head: 4 (over x).
Axes of the slice: x: 4, y: 4, z: 4 (z_hi: 2, z_lo: 2; z = z_hi * 2 + z_lo), core: 2. Of those that a mesh axis runs over, the one named last changes fastest.
Arguments:
- inputs: bfloat16 [2, 30, 480, 1536], P(None, None, 'win', 'head'), may hold values from -16 to 16
- gains: float32 [2, 1536], P('segment'), may hold values from 0.1 to 1.9
- qkv_weight: bfloat16 [2, 1536, 3, 1536], P('segment', None, None, 'head'), may hold values from -3.5 to 3.5
- out_weight: bfloat16 [2, 1536, 1536], P('segment', 'head'), may hold values from -0.15625 to 0.15625
- labels: int32 [30, 480], P(None, 'win'), may hold values from 0 to 3, as said below
Outputs:
- sections: bfloat16 [2, 2, 30, 480, 1536], P('segment', None, None, 'win', 'head')
Inputs may be any that keep to these rules, and one draw needn't show every extreme that they name: In each window of 30 by 30 cells the label is 2 on the rows from a drawn row cut on plus 1 on the columns from a drawn column cut on; both cuts lie in 1 to 29, so every window holds all four labels.
All inputs are finite; a program needn't handle non-finite values.
Results may differ from a plain program's by a relative error of at most 0.013.
Values may be sent and summed in bfloat16 or wider, within the bound.
No kernel may reach another device: no remote copies, remote signals or barrier semaphores. Data moves between devices by JAX's collectives and lax.ppermute only.
A program may use at most 128 MiB of HBM per device.

v0:
```python
import functools
import math

import jax
import jax.numpy as jnp
from jax import lax
from jax.experimental import pallas as pl
from jax.experimental.pallas import tpu as pltpu
from jax.sharding import PartitionSpec as P


D = 1536
HD = 128
HL = 3
FQ = 384
TS = 240
NT = 4 * TS
HALF = TS // 2
QROWS = 480
AROWS = 480
NEG = -1e30
QSCALE = HD**-0.5 * math.log2(math.e)
REL = (0, 3, 1, 2)
F32, BF16 = jnp.float32, jnp.bfloat16


def ring(n, by):
    return [(i, (i + by) % n) for i in range(n)]


def head_step(a, by):
    return lax.ppermute(a, "head", ring(4, by))


def set_rows(meta_ref):
    y, c = meta_ref[2], meta_ref[3]
    blocks = []
    for swapped in (False, True):
        for k in range(4):
            blocks.append(lax.rem(y + REL[k], 4) * 2 + (1 - c if swapped else c))
    return blocks


def attend_kernel(section, *refs):
    meta_ref, xparts = refs[0], refs[1:9]
    masks, refs = (refs[9:10], refs[10:]) if section == 0 else (refs[9:11], refs[11:])
    gain_ref, other_gain_ref, wown, wparts, outs, refs = refs[0], refs[1], refs[2], refs[3:11], refs[11:15], refs[15:]
    if section == 0:
        v_ref, xs, q_s, k_s, u_s, w_s, s_s, a_s, sem = refs
    else:
        xs, q_s, k_s, u_s, w_s, s_s, a_s, sem = refs
    use_own = meta_ref[0] == section
    me = meta_ref[1]

    def own_copies():
        return [pltpu.make_async_copy(wown.at[j], w_s.at[:, pl.ds(j * FQ, FQ)], sem.at[j]) for j in range(3)]

    @pl.when(use_own)
    def _():
        for copy in own_copies():
            copy.start()

    @pl.when(jnp.logical_not(use_own))
    def _():
        for block, ref in zip(set_rows(meta_ref), wparts):
            for j in range(3):
                w_s[pl.ds(pl.multiple_of(block * 192, 192), 192), FQ * j : FQ * (j + 1)] = ref[j]

    if section == 0:
        for r in range(4):
            lanes = pl.ds(pl.multiple_of(lax.rem(me + REL[r], 4) * FQ, FQ), FQ)
            xs[0 : NT // 2, lanes] = xparts[2 * r][...]
            xs[NT // 2 : NT, lanes] = xparts[2 * r + 1][...]
        v_ref[...] = xs[pl.ds(pl.multiple_of(me * TS, TS), TS), :]
    gain = jnp.where(use_own, gain_ref[...], other_gain_ref[...])
    if section == 1:
        for i in range(8):
            xs[i * HALF : (i + 1) * HALF, :] = xparts[i][...]
    for h in range(HL):
        u_s[h, :, HD:] = jnp.ones((NT, HD), BF16)

    @pl.when(use_own)
    def _():
        for copy in own_copies():
            copy.wait()

    def make_qkv(i, carry):
        rows = pl.ds(pl.multiple_of(i * QROWS, QROWS), QROWS)
        x = xs[rows, :].astype(F32)
        ms = jnp.mean(x * x, axis=-1, keepdims=True)
        normed = (x * lax.rsqrt(ms + 1e-05) * gain).astype(BF16)
        acc = jnp.dot(normed, w_s[...], preferred_element_type=F32)
        for h in range(HL):
            q_s[h, rows, :] = (acc[:, HD * h : HD * (h + 1)] * QSCALE).astype(BF16)
            k_s[h, rows, :] = acc[:, FQ + HD * h : FQ + HD * (h + 1)].astype(BF16)
            u_s[h, rows, :HD] = acc[:, 2 * FQ + HD * h : 2 * FQ + HD * (h + 1)].astype(BF16)
        return carry

    lax.fori_loop(0, NT // QROWS, make_qkv, 0)

    def score(r, h):
        rows = pl.ds(pl.multiple_of(r * AROWS, AROWS), AROWS)
        s = lax.dot_general(q_s[h, rows, :], k_s[h], (((1,), (1,)), ((), ())), preferred_element_type=F32)
        if section == 0:
            return s + masks[0][...]
        return jnp.where(masks[1][rows, :] == masks[0][...], s, NEG)

    def weigh(r, h, s):
        rows = pl.ds(pl.multiple_of(r * AROWS, AROWS), AROWS)
        p = jnp.exp2(s - jnp.max(s, axis=-1, keepdims=True)).astype(BF16)
        o = jnp.dot(p, u_s[h], preferred_element_type=F32)
        a_s[rows, HD * h : HD * (h + 1)] = (o[:, :HD] / o[:, HD:]).astype(BF16)

    s_s[...] = score(0, 0)

    def attend_rows(r, carry):
        for h in range(HL):
            now = s_s[...]
            s_s[...] = score(r, h + 1) if h + 1 < HL else score(jnp.minimum(r + 1, NT // AROWS - 1), 0)
            weigh(r, h, now)
        return carry

    lax.fori_loop(0, NT // AROWS, attend_rows, 0)
    for r in range(4):
        if section == 0:
            outs[r][...] = a_s[pl.ds(pl.multiple_of(lax.rem(me + REL[r], 4) * TS, TS), TS), :]
        else:
            outs[r][...] = a_s[r * TS : (r + 1) * TS, :]


VM = pl.BlockSpec(memory_space=pltpu.VMEM)
SM = pl.BlockSpec(memory_space=pltpu.SMEM)


def attend(section, meta, pieces, masks, gains, wown, wparts):
    shard = jax.ShapeDtypeStruct((TS, FQ), BF16)
    out_shape = [shard] * 4 + ([jax.ShapeDtypeStruct((TS, D), BF16)] if section == 0 else [])
    scratch = [
        pltpu.VMEM((NT, D), BF16),
        pltpu.VMEM((HL, NT, HD), BF16),
        pltpu.VMEM((HL, NT, HD), BF16),
        pltpu.VMEM((HL, NT, 2 * HD), BF16),
        pltpu.VMEM((D, 3 * FQ), BF16),
        pltpu.VMEM((AROWS, NT), F32),
        pltpu.VMEM((NT, FQ), BF16),
        pltpu.SemaphoreType.DMA((3,)),
    ]
    return pl.pallas_call(
        functools.partial(attend_kernel, section),
        out_shape=out_shape,
        in_specs=[SM] + [VM] * (10 + len(masks)) + [pl.BlockSpec(memory_space=pltpu.HBM)] + [VM] * 8,
        out_specs=[VM] * len(out_shape),
        scratch_shapes=scratch,
        compiler_params=pltpu.CompilerParams(vmem_limit_bytes=30 << 20),
    )(meta, *pieces, *masks, *gains, pltpu.with_memory_space_constraint(wown, pltpu.HBM), *wparts)


def project_kernel(section, meta_ref, *refs):
    att, vparts, wparts = refs[:4], refs[4:6], refs[6:14]
    outs, (w_s, a_s, t_s) = refs[14:-3], refs[-3:]
    me = meta_ref[1]
    for block, ref in zip(set_rows(meta_ref), wparts):
        for r in range(4):
            w_s[pl.ds(pl.multiple_of(block * 48 + r * FQ, 16), 48), :] = ref[r]
    for r in range(4):
        a_s[:, r * FQ : (r + 1) * FQ] = att[r][...]
    acc = jnp.dot(a_s[...], w_s[...], preferred_element_type=F32)
    for i in range(2):
        rows = slice(i * HALF, (i + 1) * HALF)
        t_s[rows, :] = (acc[rows, :] + vparts[i][...].astype(F32)).astype(BF16)
        if section == 0:
            outs[i][...] = t_s[rows, :]
    for r in range(4):
        q = lax.rem(me + REL[r], 4)
        piece = t_s[:, pl.ds(pl.multiple_of(q * FQ, FQ), FQ)]
        outs[(2 if section == 0 else 0) + r][...] = piece


def project(section, meta, att, vparts, wparts):
    out_shape = [jax.ShapeDtypeStruct((TS, FQ), BF16)] * 4
    if section == 0:
        out_shape = [jax.ShapeDtypeStruct((HALF, D), BF16)] * 2 + out_shape
    return pl.pallas_call(
        functools.partial(project_kernel, section),
        out_shape=out_shape,
        in_specs=[SM] + [VM] * 14,
        out_specs=[VM] * len(out_shape),
        scratch_shapes=[pltpu.VMEM((D, D), BF16), pltpu.VMEM((TS, D), BF16), pltpu.VMEM((TS, D), BF16)],
        compiler_params=pltpu.CompilerParams(vmem_limit_bytes=20 << 20),
    )(meta, *att, *vparts, *wparts)


def gather_head(a, b):
    parts = {}
    for key, part, by in (("la", a, 1), ("lb", b, 1), ("ra", a, -1), ("rb", b, -1)):
        parts[key] = head_step(part, by)
    oa = head_step(parts["la"], 1)
    ob = head_step(parts["rb"], -1)
    return a, b, parts["la"], parts["lb"], parts["ra"], parts["rb"], oa, ob


def exchange_head(own, to_left, to_right, to_opp):
    from_left = head_step(to_right, 1)
    from_right = head_step(to_left, -1)
    from_opp = head_step(to_opp, 2)
    return own, from_left, from_right, from_opp


def pack_kernel(*refs):
    for i in range(4):
        refs[4][i] = refs[i][...]


def pack(parts):
    return pl.pallas_call(
        pack_kernel,
        out_shape=jax.ShapeDtypeStruct((4, *parts[0].shape), parts[0].dtype),
        in_specs=[VM] * 4,
        out_specs=VM,
        name="pack",
    )(*parts)


def win_step(a, by):
    return lax.ppermute(a, "win", ring(16, by))


def gather_win(own):
    mine = [own]
    for by in (4, -4, 8):
        mine.append(win_step(own, by))
    swapped = []
    for a in mine:
        swapped.append(lax.ppermute(a, "win", [(j, j ^ 1) for j in range(16)]))
    return mine + swapped


def slot_groups(a, fill):
    pad = [(0, 0), (0, 1)] + [(0, 0)] * (a.ndim - 2)
    return (
        a[:, 0:8],
        jnp.pad(a[:, 8:15], pad, constant_values=fill),
        a[:, 15:23],
        jnp.pad(a[:, 23:30], pad, constant_values=fill),
    )


FIRST, WIDTH = (0, 8, 15, 23), (8, 7, 8, 7)


def finish_kernel(meta_ref, *refs):
    near, distant, far, local, out, g_s = refs[0], refs[1], refs[2:6], refs[6:10], refs[10], refs[11]
    seg, me = meta_ref[0], meta_ref[1]

    @pl.when(seg == 0)
    def _():
        for r in range(4):
            g = lax.rem(me + REL[r], 4)
            g_s[0, g] = near[r]
            g_s[1, g] = distant[r]

    @pl.when(seg == 1)
    def _():
        for r in range(4):
            g = lax.rem(me + REL[r] + 2, 4)
            g_s[0, g] = far[r][...]
            g_s[1, g] = local[r][...]

    for m in range(2):
        for g in range(4):
            cells = g_s[m, g].reshape(30, 8, FQ)
            out[m, :, FIRST[g] : FIRST[g] + WIDTH[g], :] = cells[:, : WIDTH[g], :]


def finish(meta, near, distant, far, local):
    return pl.pallas_call(
        finish_kernel,
        out_shape=jax.ShapeDtypeStruct((2, 30, 30, FQ), BF16),
        in_specs=[SM] + [VM] * 10,
        out_specs=VM,
        scratch_shapes=[pltpu.VMEM((2, 4, TS, FQ), BF16)],
        name="finish",
    )(meta, near, distant, *far, *local)


def pair_perm(source, target, by):
    return [(source * 4 + i, target * 4 + (i + by) % 4) for i in range(4)]


def across(a, source, target, by):
    return lax.ppermute(a, ("segment", "head"), pair_perm(source, target, by))


def deliver(pieces, source, target):
    own, to_left, to_right, to_opp = pieces
    if source != target:
        own = across(own, source, target, 0)
    from_left = across(to_right, source, target, 1)
    from_right = across(to_left, source, target, -1)
    from_opp = across(to_opp, source, target, 2)
    return own, from_left, from_right, from_opp


def program(inputs, gains, qkv_weight, out_weight, labels):
    seg = lax.axis_index("segment")
    win = lax.axis_index("win")
    me = lax.axis_index("head")
    meta = jnp.stack([seg, me, win // 4, win % 2]).astype(jnp.int32)
    block = (win // 4) * 2 + win % 2

    wown = qkv_weight[0].transpose(1, 0, 2)
    wpart = lax.dynamic_slice_in_dim(wown, block * 192, 192, 1)
    wother = lax.ppermute(wpart, "segment", ring(2, 1))
    wparts = gather_win(wother)
    gains = (gains, lax.ppermute(gains, "segment", ring(2, 1)))
    opart = lax.dynamic_slice_in_dim(out_weight[0], block * 48, 48, 0)
    oown = jnp.stack(exchange_head(opart, opart, opart, opart))
    oother = lax.ppermute(oown, "segment", ring(2, 1))
    out0 = gather_win(jnp.where(seg == 0, oown, oother))
    out1 = gather_win(jnp.where(seg == 0, oother, oown))

    x = slot_groups(lax.dynamic_index_in_dim(inputs, seg, 0, keepdims=False), 0)
    xa, xb = jnp.concatenate(x[:2]).reshape(NT // 2, FQ), jnp.concatenate(x[2:]).reshape(NT // 2, FQ)
    slot = lax.broadcasted_iota(jnp.int32, (1, NT), 1)
    real = (slot % 8 != 7) | ((slot // TS) % 2 == 0)
    padr = jnp.where(real, 0.0, NEG).astype(F32)
    *att, v = attend(0, meta, gather_head(xa, xb), (padr,), gains, wown, wparts)
    att = exchange_head(*att)
    ta, tb, *fp = project(0, meta, att, (v[:HALF], v[HALF:]), out0)

    perm = [(((w + 1) % 16) * 4 + i, w * 4 + i) for w in range(16) for i in (0, 1)]
    ta = jnp.where(me < 2, lax.ppermute(ta, ("win", "head"), perm), ta)
    tb = jnp.where(me < 2, lax.ppermute(tb, ("win", "head"), perm), tb)
    lab = jnp.stack(slot_groups(labels.astype(F32), -1.0)).reshape(4, TS)
    lab = lax.dynamic_slice_in_dim(jnp.concatenate([lab] * 3), lax.rem(me + 2, 4), 4, 0)
    lab = jnp.stack([lab[0], lab[3], lab[1], lab[2]]).reshape(NT)
    att1 = attend(1, meta, gather_head(ta, tb), (lab[None, :], lab[:, None]), gains, wown, wparts)
    att1 = exchange_head(*att1)
    sp = project(1, meta, att1, (ta, tb), out1)

    near = pack(exchange_head(*fp))
    distant = across(near, 1, 0, 0)
    s_far = deliver(sp, 0, 1)
    s_local = deliver(sp, 1, 1)
    return finish(meta, near, distant, s_far, s_local)[None]


def solution(mesh):
    in_specs = (
        P(None, None, "win", "head"),
        P("segment", None),
        P("segment", None, None, "head"),
        P("segment", "head", None),
        P(None, "win"),
    )
    out_specs = P("segment", None, None, "win", "head")
    return jax.shard_map(program, mesh=mesh, in_specs=in_specs, out_specs=out_specs, check_vma=False)
```

profile of v0, /device:TPU:98, one launch (start us, length us, event | category | flops | bytes accessed | tf_op | source)
XLA Modules:
  0.0 260.8 jit_solution(8853583778823124998)
XLA Ops:
  25.6 3.9 %collective-permute-done.refs_3_ = bf16[480,384]{1,0:T(8,128)(2,1)} collective-permute-done((bf16[480,384]{1,0:T(8,128)(2,1)S(1)}, bf16[480,384]{1,0:T(8,128)(2,1)}, u32[]{:S(2)}, u32[]{:S(2)}) %collective-permute-start) | collective-permute-done | bytes 368672 | tf_op jit(solution)/shard_map/ppermute | solution.py:32
  33.4 7.6 %collective-permute-done.2.refs_5_ = bf16[480,384]{1,0:T(8,128)(2,1)S(1)} collective-permute-done((bf16[480,384]{1,0:T(8,128)(2,1)S(1)}, bf16[480,384]{1,0:T(8,128)(2,1)S(1)}, u32[]{:S(2)}, u32[]{:S(2)}) %collective-permute-start.2) | collective-permute-done | bytes 368672 | tf_op jit(solution)/shard_map/ppermute | solution.py:32
  42.3 3.3 %collective-permute-done.5.refs_8_ = bf16[480,384]{1,0:T(8,128)(2,1)} collective-permute-done((bf16[480,384]{1,0:T(8,128)(2,1)S(1)}, bf16[480,384]{1,0:T(8,128)(2,1)}, u32[]{:S(2)}, u32[]{:S(2)}) %collective-permute-start.5) | collective-permute-done | bytes 368672 | tf_op jit(solution)/shard_map/ppermute | solution.py:32
  45.6 3.2 %collective-permute-start.10 = (bf16[3,192,384]{2,1,0:T(8,128)(2,1)S(1)}, bf16[3,192,384]{2,1,0:T(8,128)(2,1)}, u32[]{:S(2)}, u32[]{:S(2)}) collective-permute-start(bf16[3,192,384]{2,1,0:T(8,128)(2,1)S(1)} %collective-permute-done.7.refs_13_.refs_14_), channel_id=1, source_target_pairs={{0,32},{4,36},{8,40},{12,44},{16,48},{20,52},{24,56},{28,60},{32,0... | collective-permute-start | bytes 1327112 | tf_op jit(solution)/shard_map/ppermute | solution.py:225
  52.3 5.0 %collective-permute-done.10.refs_16_.refs_17_ = bf16[3,192,384]{2,1,0:T(8,128)(2,1)} collective-permute-done((bf16[3,192,384]{2,1,0:T(8,128)(2,1)S(1)}, bf16[3,192,384]{2,1,0:T(8,128)(2,1)}, u32[]{:S(2)}, u32[]{:S(2)}) %collective-permute-start.10) | collective-permute-done | bytes 442400 | tf_op jit(solution)/shard_map/ppermute | solution.py:225
  73.1 11.7 %shard_map.55 = (bf16[240,384]{1,0:T(8,128)(2,1)S(1)}, bf16[240,384]{1,0:T(8,128)(2,1)S(1)}, bf16[240,384]{1,0:T(8,128)(2,1)S(1)}, bf16[240,384]{1,0:T(8,128)(2,1)S(1)}, bf16[240,1536]{1,0:T(8,128)(2,1)S(1)}) custom-call(s32[4]{0:T(128)S(1)} %pad_add_fusion.refs_0_.meta_ref, bf16[480,384]{1,0:T(8,128)(2,1)S(1)} %copy-done.13, ...), custom_call_target="tpu_custom_call" | custom-call | tf_op jit(solution)/shard_map/pallas_call | solution.py:148
  88.0 4.2 %collective-permute-done.15.refs_1_ = bf16[240,384]{1,0:T(8,128)(2,1)S(1)} collective-permute-done((bf16[240,384]{1,0:T(8,128)(2,1)S(1)}, bf16[240,384]{1,0:T(8,128)(2,1)S(1)}, u32[]{:S(2)}, u32[]{:S(2)}) %collective-permute-start.15) | collective-permute-done | bytes 184352 | tf_op jit(solution)/shard_map/ppermute | solution.py:32
  94.8 4.9 %collective-permute-done.17.refs_3_ = bf16[240,384]{1,0:T(8,128)(2,1)S(1)} collective-permute-done((bf16[240,384]{1,0:T(8,128)(2,1)S(1)}, bf16[240,384]{1,0:T(8,128)(2,1)S(1)}, u32[]{:S(2)}, u32[]{:S(2)}) %collective-permute-start.17) | collective-permute-done | bytes 184352 | tf_op jit(solution)/shard_map/ppermute | solution.py:32
  99.8 4.1 %shard_map.56 = (bf16[120,1536]{1,0:T(8,128)(2,1)S(1)}, bf16[120,1536]{1,0:T(8,128)(2,1)}, bf16[240,384]{1,0:T(8,128)(2,1)S(1)}, bf16[240,384]{1,0:T(8,128)(2,1)...) custom-call(s32[4]{0:T(128)S(1)} %pad_add_fusion.refs_0_.meta_ref, ...), custom_call_target="tpu_custom_call" | custom-call | tf_op jit(solution)/shard_map/pallas_call | solution.py:183
  116.1 5.1 %collective-permute-done.33 = bf16[120,1536]{1,0:T(8,128)(2,1)S(1)} collective-permute-done((bf16[120,1536]{1,0:T(8,128)(2,1)}, bf16[120,1536]{1,0:T(8,128)(2,1)S(1)}, u32[]{:S(2)}, u32[]{:S(2)}) %collective-permute-start.33) | collective-permute-done | bytes 368672 | tf_op jit(solution)/shard_map/ppermute | solution.py:332
  124.0 15.2 %collective-permute-done.44.refs_7_ = bf16[4,48,1536]{2,1,0:T(8,128)(2,1)} collective-permute-done((bf16[4,48,1536]{2,1,0:T(8,128)(2,1)S(1)}, bf16[4,48,1536]{2,1,0:T(8,128)(2,1)}, u32[]{:S(2)}, u32[]{:S(2)}) %collective-permute-start.44) | collective-permute-done | bytes 589856 | tf_op jit(solution)/shard_map/ppermute | solution.py:225
  141.9 3.2 %collective-permute-start.37 = (bf16[120,1536]{1,0:T(8,128)(2,1)S(1)}, bf16[120,1536]{1,0:T(8,128)(2,1)S(1)}, u32[]{:S(2)}, u32[]{:S(2)}) collective-permute-start(bf16[120,1536]{1,0:T(8,128)(2,1)S(1)} %broadcast_select_fusion.3.refs_1_.refs_4_), channel_id=1, source_target_pairs={{0,3},{1,0},{2,1},{3,2},{4,7},{5,4},{6,5},{7,6},{8,11},{9,8},{10,9... | collective-permute-start | bytes 1105928 | tf_op jit(solution)/shard_map/ppermute | solution.py:32
  145.2 5.5 %collective-permute-start.31 = (bf16[240,384]{1,0:T(8,128)(2,1)S(1)}, bf16[240,384]{1,0:T(8,128)(2,1)S(1)}, u32[]{:S(2)}, u32[]{:S(2)}) collective-permute-start(bf16[240,384]{1,0:T(8,128)(2,1)S(1)} %copy-done.36), channel_id=1, source_target_pairs={{0,2},{1,3},{2,0},{3,1},{4,6},{5,7},{6,4},{7,5},{8,10},{9,11},{10,... | collective-permute-start | bytes 552968 | tf_op jit(solution)/shard_map/ppermute | solution.py:32
  152.7 4.8 %collective-permute-done.31.refs_3_ = bf16[240,384]{1,0:T(8,128)(2,1)S(1)} collective-permute-done((bf16[240,384]{1,0:T(8,128)(2,1)S(1)}, bf16[240,384]{1,0:T(8,128)(2,1)S(1)}, u32[]{:S(2)}, u32[]{:S(2)}) %collective-permute-start.31) | collective-permute-done | bytes 184352 | tf_op jit(solution)/shard_map/ppermute | solution.py:32
  157.5 11.0 %collective-permute-start.47 = (bf16[4,48,1536]{2,1,0:T(8,128)(2,1)S(1)}, bf16[4,48,1536]{2,1,0:T(8,128)(2,1)}, u32[]{:S(2)}, u32[]{:S(2)}) collective-permute-start(bf16[4,48,1536]{2,1,0:T(8,128)(2,1)S(1)} %get-tuple-element.43.refs_6_), channel_id=1, source_target_pairs={{0,4},{4,0},{8,12},{12,8},{16,20},{20,16},{24,28},{28,24},{32,36},... | collective-permute-start | bytes 1769480 | tf_op jit(solution)/shard_map/ppermute | solution.py:234
  172.8 6.9 %collective-permute-start.32 = (bf16[4,240,384]{2,1,0:T(8,128)(2,1)}, bf16[4,240,384]{2,1,0:T(8,128)(2,1)}, u32[]{:S(2)}, u32[]{:S(2)}) collective-permute-start(bf16[4,240,384]{2,1,0:T(8,128)(2,1)} %pack.1.refs_0_), channel_id=1, source_target_pairs={{64,0},{65,1},{66,2},{67,3},{68,4},{69,5},{70,6},{71,7},{72,8},{73... | collective-permute-start | bytes 2211848 | tf_op jit(solution)/shard_map/ppermute | solution.py:291
  188.6 13.1 %shard_map.57 = (bf16[240,384]{1,0:T(8,128)(2,1)S(1)}, bf16[240,384]{1,0:T(8,128)(2,1)S(1)}, bf16[240,384]{1,0:T(8,128)(2,1)S(1)}, bf16[240,384]{1,0:T(8,128)(2,1)S(1)}) custom-call(s32[4]{0:T(128)S(1)} %pad_add_fusion.refs_0_.meta_ref, bf16[120,1536]{1,0:T(8,128)(2,1)S(1)} %broadcast_select_fusion.3.refs_1_.refs_4_, ...), custom_call_target="tpu_custom_call" | custom-call | tf_op jit(solution)/shard_map/pallas_call | solution.py:148
  204.2 4.3 %collective-permute-start.43 = (bf16[240,384]{1,0:T(8,128)(2,1)S(1)}, bf16[240,384]{1,0:T(8,128)(2,1)S(1)}, u32[]{:S(2)}, u32[]{:S(2)}) collective-permute-start(bf16[240,384]{1,0:T(8,128)(2,1)S(1)} %get-tuple-element.38), channel_id=1, source_target_pairs={{0,2},{1,3},{2,0},{3,1},{4,6},{5,7},{6,4},{7,5},{8,10},{9,11},{10,... | collective-permute-start | bytes 552968 | tf_op jit(solution)/shard_map/ppermute | solution.py:32
  211.5 4.8 %collective-permute-done.43.refs_3_ = bf16[240,384]{1,0:T(8,128)(2,1)S(1)} collective-permute-done((bf16[240,384]{1,0:T(8,128)(2,1)S(1)}, bf16[240,384]{1,0:T(8,128)(2,1)S(1)}, u32[]{:S(2)}, u32[]{:S(2)}) %collective-permute-start.43) | collective-permute-done | bytes 184352 | tf_op jit(solution)/shard_map/ppermute | solution.py:32
  216.3 3.9 %shard_map.58 = (bf16[240,384]{1,0:T(8,128)(2,1)S(1)}, bf16[240,384]{1,0:T(8,128)(2,1)S(1)}, bf16[240,384]{1,0:T(8,128)(2,1)S(1)}, bf16[240,384]{1,0:T(8,128)(2,1)S(1)}) custom-call(s32[4]{0:T(128)S(1)} %pad_add_fusion.refs_0_.meta_ref, bf16[240,384]{1,0:T(8,128)(2,1)S(1)} %get-tuple-element.35.refs_0_, ...), custom_call_target="tpu_custom_call" | custom-call | tf_op jit(solution)/shard_map/pallas_call | solution.py:183
  227.3 13.5 %collective-permute-done.51.refs_2_ = bf16[240,384]{1,0:T(8,128)(2,1)S(1)} collective-permute-done((bf16[240,384]{1,0:T(8,128)(2,1)S(1)}, bf16[240,384]{1,0:T(8,128)(2,1)S(1)}, u32[]{:S(2)}, u32[]{:S(2)}) %collective-permute-start.51) | collective-permute-done | bytes 184352 | tf_op jit(solution)/shard_map/ppermute | solution.py:291
  248.2 4.5 %collective-permute-done.57.refs_9_ = bf16[240,384]{1,0:T(8,128)(2,1)S(1)} collective-permute-done((bf16[240,384]{1,0:T(8,128)(2,1)S(1)}, bf16[240,384]{1,0:T(8,128)(2,1)S(1)}, u32[]{:S(2)}, u32[]{:S(2)}) %collective-permute-start.57) | collective-permute-done | bytes 184352 | tf_op jit(solution)/shard_map/ppermute | solution.py:291
  253.5 3.5 %finish.1 = bf16[2,30,30,384]{3,2,1,0:T(8,128)(2,1)} custom-call(s32[4]{0:T(128)} %copy-done.34, bf16[4,240,384]{2,1,0:T(8,128)(2,1)} %pack.1.refs_0_, bf16[4,240,384]{2,1,0:T(8,128)(2,1)} %collective-permute-done.32.refs_1_, bf16[240,384]{1,0:T(8,128)(2,1)} %copy-done.46, bf16[240,384]{1,0:T(8,128)(2,1)} %copy-done.47, bf16[240,384]{1,0:T(8,128)(2,1)} %copy-done.49, ...), custom_call_target="tpu_custom_call" | custom-call | tf_op jit(solution)/shard_map/finish/pallas_call | solution.py:276
  257.0 3.9 %copy.9 = bf16[1,2,30,30,384]{4,1,3,2,0:T(2,128)(2,1)} copy(bf16[1,2,30,30,384]{4,3,2,1,0:T(8,128)(2,1)} %bitcast.26) | data formatting | bytes 2764800 | tf_op jit(solution)/shard_map/broadcast_in_dim | solution.py:345
  (238 shorter events, 109.3 us)
Async XLA Ops:
  20.6 28.2 %collective-permute-start.21 = (bf16[4,48,1536]{2,1,0:T(8,128)(2,1)}, bf16[4,48,1536]{2,1,0:T(8,128)(2,1)}, u32[]{:S(2)}, u32[]{:S(2)}) collective-permute-start(bf16[4,48,1536]{2,1,0:T(8,128)(2,1)} %pad_maximum_fusion), channel_id=1, source_target_pairs={{0,64},{64,0},{1,65},{65,1},{2,66},{66,2},{3,67},{67,3},{4,68},{68... | collective-permute-start | bytes 1769480 | tf_op jit(solution)/shard_map/ppermute | solution.py:318
  22.4 26.4 %collective-permute-start.8 = (bf16[3,192,384]{2,1,0:T(8,128)(2,1)S(1)}, bf16[3,192,384]{2,1,0:T(8,128)(2,1)}, u32[]{:S(2)}, u32[]{:S(2)}) collective-permute-start(bf16[3,192,384]{2,1,0:T(8,128)(2,1)S(1)} %collective-permute-done.7.refs_13_.refs_14_), channel_id=1, source_target_pairs={{0,16},{4,20},{8,24},{12,28},{16,32},{20,36},{24,40},{28,44},{32,4... | collective-permute-start | bytes 1327112 | tf_op jit(solution)/shard_map/ppermute | solution.py:225
  24.0 25.3 %collective-permute-start.9 = (bf16[3,192,384]{2,1,0:T(8,128)(2,1)S(1)}, bf16[3,192,384]{2,1,0:T(8,128)(2,1)}, u32[]{:S(2)}, u32[]{:S(2)}) collective-permute-start(bf16[3,192,384]{2,1,0:T(8,128)(2,1)S(1)} %collective-permute-done.7.refs_13_.refs_14_), channel_id=1, source_target_pairs={{0,48},{4,52},{8,56},{12,60},{16,0},{20,4},{24,8},{28,12},{32,16},... | collective-permute-start | bytes 1327112 | tf_op jit(solution)/shard_map/ppermute | solution.py:225
  51.6 33.8 %collective-permute-start.22 = (bf16[4,48,1536]{2,1,0:T(8,128)(2,1)S(1)}, bf16[4,48,1536]{2,1,0:T(8,128)(2,1)}, u32[]{:S(2)}, u32[]{:S(2)}) collective-permute-start(bf16[4,48,1536]{2,1,0:T(8,128)(2,1)S(1)} %get-tuple-element.44.refs_6_), channel_id=1, source_target_pairs={{0,16},{4,20},{8,24},{12,28},{16,32},{20,36},{24,40},{28,44},{32,4... | collective-permute-start | bytes 1769480 | tf_op jit(solution)/shard_map/ppermute | solution.py:225
  57.4 28.1 %collective-permute-start.23 = (bf16[4,48,1536]{2,1,0:T(8,128)(2,1)S(1)}, bf16[4,48,1536]{2,1,0:T(8,128)(2,1)}, u32[]{:S(2)}, u32[]{:S(2)}) collective-permute-start(bf16[4,48,1536]{2,1,0:T(8,128)(2,1)S(1)} %get-tuple-element.44.refs_6_), channel_id=1, source_target_pairs={{0,48},{4,52},{8,56},{12,60},{16,0},{20,4},{24,8},{28,12},{32,16},... | collective-permute-start | bytes 1769480 | tf_op jit(solution)/shard_map/ppermute | solution.py:225
  61.0 25.0 %collective-permute-start.24 = (bf16[4,48,1536]{2,1,0:T(8,128)(2,1)S(1)}, bf16[4,48,1536]{2,1,0:T(8,128)(2,1)}, u32[]{:S(2)}, u32[]{:S(2)}) collective-permute-start(bf16[4,48,1536]{2,1,0:T(8,128)(2,1)S(1)} %get-tuple-element.44.refs_6_), channel_id=1, source_target_pairs={{0,32},{4,36},{8,40},{12,44},{16,48},{20,52},{24,56},{28,60},{32,0... | collective-permute-start | bytes 1769480 | tf_op jit(solution)/shard_map/ppermute | solution.py:225
  63.8 22.3 %collective-permute-start.25 = (bf16[4,48,1536]{2,1,0:T(8,128)(2,1)S(1)}, bf16[4,48,1536]{2,1,0:T(8,128)(2,1)}, u32[]{:S(2)}, u32[]{:S(2)}) collective-permute-start(bf16[4,48,1536]{2,1,0:T(8,128)(2,1)S(1)} %get-tuple-element.44.refs_6_), channel_id=1, source_target_pairs={{0,4},{4,0},{8,12},{12,8},{16,20},{20,16},{24,28},{28,24},{32,36},... | collective-permute-start | bytes 1769480 | tf_op jit(solution)/shard_map/ppermute | solution.py:234
  109.4 29.8 %collective-permute-start.44 = (bf16[4,48,1536]{2,1,0:T(8,128)(2,1)S(1)}, bf16[4,48,1536]{2,1,0:T(8,128)(2,1)}, u32[]{:S(2)}, u32[]{:S(2)}) collective-permute-start(bf16[4,48,1536]{2,1,0:T(8,128)(2,1)S(1)} %get-tuple-element.43.refs_6_), channel_id=1, source_target_pairs={{0,16},{4,20},{8,24},{12,28},{16,32},{20,36},{24,40},{28,44},{32,4... | collective-permute-start | bytes 1769480 | tf_op jit(solution)/shard_map/ppermute | solution.py:225
  110.9 28.3 %collective-permute-start.45 = (bf16[4,48,1536]{2,1,0:T(8,128)(2,1)S(1)}, bf16[4,48,1536]{2,1,0:T(8,128)(2,1)}, u32[]{:S(2)}, u32[]{:S(2)}) collective-permute-start(bf16[4,48,1536]{2,1,0:T(8,128)(2,1)S(1)} %get-tuple-element.43.refs_6_), channel_id=1, source_target_pairs={{0,48},{4,52},{8,56},{12,60},{16,0},{20,4},{24,8},{28,12},{32,16},... | collective-permute-start | bytes 1769480 | tf_op jit(solution)/shard_map/ppermute | solution.py:225
  112.7 29.2 %collective-permute-start.46 = (bf16[4,48,1536]{2,1,0:T(8,128)(2,1)S(1)}, bf16[4,48,1536]{2,1,0:T(8,128)(2,1)}, u32[]{:S(2)}, u32[]{:S(2)}) collective-permute-start(bf16[4,48,1536]{2,1,0:T(8,128)(2,1)S(1)} %get-tuple-element.43.refs_6_), channel_id=1, source_target_pairs={{0,32},{4,36},{8,40},{12,44},{16,48},{20,52},{24,56},{28,60},{32,0... | collective-permute-start | bytes 1769480 | tf_op jit(solution)/shard_map/ppermute | solution.py:225
  115.9 26.0 %collective-permute-start.29 = (bf16[240,384]{1,0:T(8,128)(2,1)}, bf16[240,384]{1,0:T(8,128)(2,1)S(1)}, u32[]{:S(2)}, u32[]{:S(2)}) collective-permute-start(bf16[240,384]{1,0:T(8,128)(2,1)} %copy-done.39), channel_id=1, source_target_pairs={{0,1},{1,2},{2,3},{3,0},{4,5},{5,6},{6,7},{7,4},{8,9},{9,10},{10,1... | collective-permute-start | bytes 552968 | tf_op jit(solution)/shard_map/ppermute | solution.py:32
  121.2 29.4 %collective-permute-start.38 = (bf16[120,1536]{1,0:T(8,128)(2,1)S(1)}, bf16[120,1536]{1,0:T(8,128)(2,1)S(1)}, u32[]{:S(2)}, u32[]{:S(2)}) collective-permute-start(bf16[120,1536]{1,0:T(8,128)(2,1)S(1)} %broadcast_select_fusion.2.refs_2_.refs_5_), channel_id=1, source_target_pairs={{0,3},{1,0},{2,1},{3,2},{4,7},{5,4},{6,5},{7,6},{8,11},{9,8},{10,9... | collective-permute-start | bytes 1105928 | tf_op jit(solution)/shard_map/ppermute | solution.py:32
  141.9 26.6 %collective-permute-start.36 = (bf16[120,1536]{1,0:T(8,128)(2,1)S(1)}, bf16[120,1536]{1,0:T(8,128)(2,1)S(1)}, u32[]{:S(2)}, u32[]{:S(2)}) collective-permute-start(bf16[120,1536]{1,0:T(8,128)(2,1)S(1)} %broadcast_select_fusion.2.refs_2_.refs_5_), channel_id=1, source_target_pairs={{0,1},{1,2},{2,3},{3,0},{4,5},{5,6},{6,7},{7,4},{8,9},{9,10},{10,1... | collective-permute-start | bytes 1105928 | tf_op jit(solution)/shard_map/ppermute | solution.py:32
  141.9 27.4 %collective-permute-start.37 = (bf16[120,1536]{1,0:T(8,128)(2,1)S(1)}, bf16[120,1536]{1,0:T(8,128)(2,1)S(1)}, u32[]{:S(2)}, u32[]{:S(2)}) collective-permute-start(bf16[120,1536]{1,0:T(8,128)(2,1)S(1)} %broadcast_select_fusion.3.refs_1_.refs_4_), channel_id=1, source_target_pairs={{0,3},{1,0},{2,1},{3,2},{4,7},{5,4},{6,5},{7,6},{8,11},{9,8},{10,9... | collective-permute-start | bytes 1105928 | tf_op jit(solution)/shard_map/ppermute | solution.py:32
  150.7 22.1 %collective-permute-start.40 = (bf16[120,1536]{1,0:T(8,128)(2,1)S(1)}, bf16[120,1536]{1,0:T(8,128)(2,1)}, u32[]{:S(2)}, u32[]{:S(2)}) collective-permute-start(bf16[120,1536]{1,0:T(8,128)(2,1)S(1)} %collective-permute-done.38.refs_6_), channel_id=1, source_target_pairs={{0,3},{1,0},{2,1},{3,2},{4,7},{5,4},{6,5},{7,6},{8,11},{9,8},{10,9... | collective-permute-start | bytes 1105928 | tf_op jit(solution)/shard_map/ppermute | solution.py:32
  150.7 22.1 %collective-permute-start.39 = (bf16[120,1536]{1,0:T(8,128)(2,1)S(1)}, bf16[120,1536]{1,0:T(8,128)(2,1)}, u32[]{:S(2)}, u32[]{:S(2)}) collective-permute-start(bf16[120,1536]{1,0:T(8,128)(2,1)S(1)} %collective-permute-done.35.refs_3_), channel_id=1, source_target_pairs={{0,1},{1,2},{2,3},{3,0},{4,5},{5,6},{6,7},{7,4},{8,9},{9,10},{10,1... | collective-permute-start | bytes 1105928 | tf_op jit(solution)/shard_map/ppermute | solution.py:32
  157.5 44.2 %collective-permute-start.47 = (bf16[4,48,1536]{2,1,0:T(8,128)(2,1)S(1)}, bf16[4,48,1536]{2,1,0:T(8,128)(2,1)}, u32[]{:S(2)}, u32[]{:S(2)}) collective-permute-start(bf16[4,48,1536]{2,1,0:T(8,128)(2,1)S(1)} %get-tuple-element.43.refs_6_), channel_id=1, source_target_pairs={{0,4},{4,0},{8,12},{12,8},{16,20},{20,16},{24,28},{28,24},{32,36},... | collective-permute-start | bytes 1769480 | tf_op jit(solution)/shard_map/ppermute | solution.py:234
  169.3 32.8 %collective-permute-start.48 = (bf16[4,48,1536]{2,1,0:T(8,128)(2,1)}, bf16[4,48,1536]{2,1,0:T(8,128)(2,1)}, u32[]{:S(2)}, u32[]{:S(2)}) collective-permute-start(bf16[4,48,1536]{2,1,0:T(8,128)(2,1)} %collective-permute-done.44.refs_7_), channel_id=1, source_target_pairs={{0,4},{4,0},{8,12},{12,8},{16,20},{20,16},{24,28},{28,24},{32,36},... | collective-permute-start | bytes 1769480 | tf_op jit(solution)/shard_map/ppermute | solution.py:234
  170.1 34.0 %collective-permute-start.49 = (bf16[4,48,1536]{2,1,0:T(8,128)(2,1)}, bf16[4,48,1536]{2,1,0:T(8,128)(2,1)}, u32[]{:S(2)}, u32[]{:S(2)}) collective-permute-start(bf16[4,48,1536]{2,1,0:T(8,128)(2,1)} %collective-permute-done.45.refs_8_), channel_id=1, source_target_pairs={{0,4},{4,0},{8,12},{12,8},{16,20},{20,16},{24,28},{28,24},{32,36},... | collective-permute-start | bytes 1769480 | tf_op jit(solution)/shard_map/ppermute | solution.py:234
  172.8 35.7 %collective-permute-start.50 = (bf16[4,48,1536]{2,1,0:T(8,128)(2,1)}, bf16[4,48,1536]{2,1,0:T(8,128)(2,1)}, u32[]{:S(2)}, u32[]{:S(2)}) collective-permute-start(bf16[4,48,1536]{2,1,0:T(8,128)(2,1)} %collective-permute-done.46.refs_9_), channel_id=1, source_target_pairs={{0,4},{4,0},{8,12},{12,8},{16,20},{20,16},{24,28},{28,24},{32,36},... | collective-permute-start | bytes 1769480 | tf_op jit(solution)/shard_map/ppermute | solution.py:234
  172.8 53.2 %collective-permute-start.32 = (bf16[4,240,384]{2,1,0:T(8,128)(2,1)}, bf16[4,240,384]{2,1,0:T(8,128)(2,1)}, u32[]{:S(2)}, u32[]{:S(2)}) collective-permute-start(bf16[4,240,384]{2,1,0:T(8,128)(2,1)} %pack.1.refs_0_), channel_id=1, source_target_pairs={{64,0},{65,1},{66,2},{67,3},{68,4},{69,5},{70,6},{71,7},{72,8},{73... | collective-permute-start | bytes 2211848 | tf_op jit(solution)/shard_map/ppermute | solution.py:291
  221.5 22.3 %collective-permute-start.52 = (bf16[240,384]{1,0:T(8,128)(2,1)S(1)}, bf16[240,384]{1,0:T(8,128)(2,1)S(1)}, u32[]{:S(2)}, u32[]{:S(2)}) collective-permute-start(bf16[240,384]{1,0:T(8,128)(2,1)S(1)} %get-tuple-element.40), channel_id=1, source_target_pairs={{0,65},{1,66},{2,67},{3,64},{4,69},{5,70},{6,71},{7,68},{8,73},{9,... | collective-permute-start | bytes 552968 | tf_op jit(solution)/shard_map/ppermute | solution.py:291
  222.8 23.0 %collective-permute-start.55 = (bf16[240,384]{1,0:T(8,128)(2,1)S(1)}, bf16[240,384]{1,0:T(8,128)(2,1)S(1)}, u32[]{:S(2)}, u32[]{:S(2)}) collective-permute-start(bf16[240,384]{1,0:T(8,128)(2,1)S(1)} %get-tuple-element.40), channel_id=1, source_target_pairs={{64,65},{65,66},{66,67},{67,64},{68,69},{69,70},{70,71},{71,68},{7... | collective-permute-start | bytes 552968 | tf_op jit(solution)/shard_map/ppermute | solution.py:291
  224.7 21.0 %collective-permute-start.53 = (bf16[240,384]{1,0:T(8,128)(2,1)S(1)}, bf16[240,384]{1,0:T(8,128)(2,1)S(1)}, u32[]{:S(2)}, u32[]{:S(2)}) collective-permute-start(bf16[240,384]{1,0:T(8,128)(2,1)S(1)} %get-tuple-element.41), channel_id=1, source_target_pairs={{0,67},{1,64},{2,65},{3,66},{4,71},{5,68},{6,69},{7,70},{8,75},{9,... | collective-permute-start | bytes 552968 | tf_op jit(solution)/shard_map/ppermute | solution.py:291
  (88 other events, 1053.6 us)
where the time goes:
time: 262 us; the launch traced here: 261 us
  starting transfers between devices  95.8 us (37%)
  waiting for transfers between devices  84.7 us (32%)
  Pallas kernels  38.3 us (15%)
  local copies, waits for them, and re-layouts  37.9 us (14%)
  other arithmetic  3.56 us (1%)
    ppermute x24, starting transfers between devices, head_step(): return lax.ppermute(a, 'head', ring(4, by))  38.4 us
    ppermute x24, waiting for transfers between devices, head_step(): return lax.ppermute(a, 'head', ring(4, by))  36.6 us
    unnamed x109, local copies, waits for them, and re-layouts  27.1 us
    pallas_call x2, Pallas kernels, attend(): pl.pallas_call(functools.partial(attend_kernel, section), out_shape=out_s...  24.8 us
    ppermute x8, waiting for transfers between devices, across(): return lax.ppermute(a, ('segment', 'head'), pair_perm(source, target, by))  20.4 us
    ppermute x9, waiting for transfers between devices, win_step(): return lax.ppermute(a, 'win', ring(16, by))  20.2 us
    ppermute x8, starting transfers between devices, across(): return lax.ppermute(a, ('segment', 'head'), pair_perm(source, target, by))  18.9 us
    ppermute x9, starting transfers between devices, win_step(): return lax.ppermute(a, 'win', ring(16, by))  15.6 us
  transfers between devices with their start and end apart: 58, of which 17 were waited for; matrix products, arithmetic and copies ran while one was open for 3% of the time, Pallas kernels for 12%

commit v1 on v0

--- a/solution.py
+++ b/solution.py
@@ -43,12 +43,12 @@
 
 def attend_kernel(section, *refs):
     meta_ref, xparts = refs[0], refs[1:9]
-    masks, refs = (refs[9:10], refs[10:]) if section == 0 else (refs[9:11], refs[11:])
+    masks, refs = (refs[9:10], refs[10:]) if section == 0 else (refs[9:13], refs[13:])
     gain_ref, other_gain_ref, wown, wparts, outs, refs = refs[0], refs[1], refs[2], refs[3:11], refs[11:15], refs[15:]
     if section == 0:
         v_ref, xs, q_s, k_s, u_s, w_s, s_s, a_s, sem = refs
     else:
-        xs, q_s, k_s, u_s, w_s, s_s, a_s, sem = refs
+        keep_ref, give_ref, xs, q_s, k_s, u_s, w_s, s_s, a_s, sem, g_s = refs
     use_own = meta_ref[0] == section
     me = meta_ref[1]
 
@@ -76,6 +76,17 @@
     if section == 1:
         for i in range(8):
             xs[i * HALF : (i + 1) * HALF, :] = xparts[i][...]
+
+        @pl.when(me < 2)
+        def _():
+            for i in range(2):
+                xs[i * HALF : (i + 1) * HALF, :] = masks[2 + i][...]
+
+        lanes = pl.ds(pl.multiple_of(me * FQ, FQ), FQ)
+        for r in range(4):
+            g_s[lax.rem(me + REL[r], 4)] = xs[r * TS : (r + 1) * TS, lanes]
+        give_ref[...] = g_s[:2]
+        keep_ref[...] = g_s[2:]
     for h in range(HL):
         u_s[h, :, HD:] = jnp.ones((NT, HD), BF16)
 
@@ -134,7 +145,10 @@
 
 def attend(section, meta, pieces, masks, gains, wown, wparts):
     shard = jax.ShapeDtypeStruct((TS, FQ), BF16)
-    out_shape = [shard] * 4 + ([jax.ShapeDtypeStruct((TS, D), BF16)] if section == 0 else [])
+    if section == 0:
+        out_shape = [shard] * 4 + [jax.ShapeDtypeStruct((TS, D), BF16)]
+    else:
+        out_shape = [shard] * 4 + [jax.ShapeDtypeStruct((2, TS, FQ), BF16)] * 2
     scratch = [
         pltpu.VMEM((NT, D), BF16),
         pltpu.VMEM((HL, NT, HD), BF16),
@@ -145,6 +159,8 @@
         pltpu.VMEM((NT, FQ), BF16),
         pltpu.SemaphoreType.DMA((3,)),
     ]
+    if section == 1:
+        scratch += [pltpu.VMEM((4, TS, FQ), BF16)]
     return pl.pallas_call(
         functools.partial(attend_kernel, section),
         out_shape=out_shape,
@@ -156,8 +172,9 @@
 
 
 def project_kernel(section, meta_ref, *refs):
-    att, vparts, wparts = refs[:4], refs[4:6], refs[6:14]
-    outs, (w_s, a_s, t_s) = refs[14:-3], refs[-3:]
+    n = 6 if section == 0 else 8
+    att, vparts, wparts = refs[:4], refs[4:n], refs[n : n + 8]
+    outs, (w_s, a_s, t_s) = refs[n + 8 : -3], refs[-3:]
     me = meta_ref[1]
     for block, ref in zip(set_rows(meta_ref), wparts):
         for r in range(4):
@@ -167,36 +184,40 @@
     acc = jnp.dot(a_s[...], w_s[...], preferred_element_type=F32)
     for i in range(2):
         rows = slice(i * HALF, (i + 1) * HALF)
-        t_s[rows, :] = (acc[rows, :] + vparts[i][...].astype(F32)).astype(BF16)
+        v = vparts[i][...].astype(F32)
+        if section == 1:
+            v = jnp.where(me < 2, vparts[2 + i][...].astype(F32), v)
+        t_s[rows, :] = (acc[rows, :] + v).astype(BF16)
         if section == 0:
             outs[i][...] = t_s[rows, :]
-    for r in range(4):
-        q = lax.rem(me + REL[r], 4)
-        piece = t_s[:, pl.ds(pl.multiple_of(q * FQ, FQ), FQ)]
-        outs[(2 if section == 0 else 0) + r][...] = piece
+    if section == 1:
+        for r in range(4):
+            q = lax.rem(me + REL[r], 4)
+            outs[r][...] = t_s[:, pl.ds(pl.multiple_of(q * FQ, FQ), FQ)]
 
 
 def project(section, meta, att, vparts, wparts):
-    out_shape = [jax.ShapeDtypeStruct((TS, FQ), BF16)] * 4
     if section == 0:
-        out_shape = [jax.ShapeDtypeStruct((HALF, D), BF16)] * 2 + out_shape
+        out_shape = [jax.ShapeDtypeStruct((HALF, D), BF16)] * 2
+    else:
+        out_shape = [jax.ShapeDtypeStruct((TS, FQ), BF16)] * 4
     return pl.pallas_call(
         functools.partial(project_kernel, section),
         out_shape=out_shape,
-        in_specs=[SM] + [VM] * 14,
+        in_specs=[SM] + [VM] * (12 + len(vparts)),
         out_specs=[VM] * len(out_shape),
         scratch_shapes=[pltpu.VMEM((D, D), BF16), pltpu.VMEM((TS, D), BF16), pltpu.VMEM((TS, D), BF16)],
         compiler_params=pltpu.CompilerParams(vmem_limit_bytes=20 << 20),
     )(meta, *att, *vparts, *wparts)
 
 
-def gather_head(a, b):
+def gather_head(a, b, step):
     parts = {}
     for key, part, by in (("la", a, 1), ("lb", b, 1), ("ra", a, -1), ("rb", b, -1)):
-        parts[key] = head_step(part, by)
+        parts[key] = step(part, by)
     oa = head_step(parts["la"], 1)
     ob = head_step(parts["rb"], -1)
-    return a, b, parts["la"], parts["lb"], parts["ra"], parts["rb"], oa, ob
+    return parts["la"], parts["lb"], parts["ra"], parts["rb"], oa, ob
 
 
 def exchange_head(own, to_left, to_right, to_opp):
@@ -204,21 +225,6 @@
     from_right = head_step(to_left, -1)
     from_opp = head_step(to_opp, 2)
     return own, from_left, from_right, from_opp
-
-
-def pack_kernel(*refs):
-    for i in range(4):
-        refs[4][i] = refs[i][...]
-
-
-def pack(parts):
-    return pl.pallas_call(
-        pack_kernel,
-        out_shape=jax.ShapeDtypeStruct((4, *parts[0].shape), parts[0].dtype),
-        in_specs=[VM] * 4,
-        out_specs=VM,
-        name="pack",
-    )(*parts)
 
 
 def win_step(a, by):
@@ -249,15 +255,14 @@
 
 
 def finish_kernel(meta_ref, *refs):
-    near, distant, far, local, out, g_s = refs[0], refs[1], refs[2:6], refs[6:10], refs[10], refs[11]
+    near, distant, far, local, out, g_s = refs[:2], refs[2:4], refs[4:8], refs[8:12], refs[12], refs[13]
     seg, me = meta_ref[0], meta_ref[1]
 
     @pl.when(seg == 0)
     def _():
-        for r in range(4):
-            g = lax.rem(me + REL[r], 4)
-            g_s[0, g] = near[r]
-            g_s[1, g] = distant[r]
+        for i in range(2):
+            g_s[0, 2 * i : 2 * i + 2] = near[i][...]
+            g_s[1, 2 * i : 2 * i + 2] = distant[i][...]
 
     @pl.when(seg == 1)
     def _():
@@ -276,11 +281,11 @@
     return pl.pallas_call(
         finish_kernel,
         out_shape=jax.ShapeDtypeStruct((2, 30, 30, FQ), BF16),
-        in_specs=[SM] + [VM] * 10,
+        in_specs=[SM] + [VM] * 12,
         out_specs=VM,
         scratch_shapes=[pltpu.VMEM((2, 4, TS, FQ), BF16)],
         name="finish",
-    )(meta, near, distant, *far, *local)
+    )(meta, *near, *distant, *far, *local)
 
 
 def pair_perm(source, target, by):
@@ -324,25 +329,35 @@
     slot = lax.broadcasted_iota(jnp.int32, (1, NT), 1)
     real = (slot % 8 != 7) | ((slot // TS) % 2 == 0)
     padr = jnp.where(real, 0.0, NEG).astype(F32)
-    *att, v = attend(0, meta, gather_head(xa, xb), (padr,), gains, wown, wparts)
+    *att, v = attend(0, meta, (xa, xb, *gather_head(xa, xb, head_step)), (padr,), gains, wown, wparts)
     att = exchange_head(*att)
-    ta, tb, *fp = project(0, meta, att, (v[:HALF], v[HALF:]), out0)
-
-    perm = [(((w + 1) % 16) * 4 + i, w * 4 + i) for w in range(16) for i in (0, 1)]
-    ta = jnp.where(me < 2, lax.ppermute(ta, ("win", "head"), perm), ta)
-    tb = jnp.where(me < 2, lax.ppermute(tb, ("win", "head"), perm), tb)
+    ta, tb = project(0, meta, att, (v[:HALF], v[HALF:]), out0)
+
+    def source(w, i):
+        return ((w + 1) % 16 if i < 2 else w) * 4 + i
+
+    def shifted_step(part, by):
+        perm = [(source(w, i), w * 4 + (i + by) % 4) for w in range(16) for i in range(4)]
+        return lax.ppermute(part, ("win", "head"), perm)
+
+    others = gather_head(ta, tb, shifted_step)
+    perm = [(source(w, i), w * 4 + i) for w in range(16) for i in (0, 1)]
+    sa = lax.ppermute(ta, ("win", "head"), perm)
+    sb = lax.ppermute(tb, ("win", "head"), perm)
     lab = jnp.stack(slot_groups(labels.astype(F32), -1.0)).reshape(4, TS)
     lab = lax.dynamic_slice_in_dim(jnp.concatenate([lab] * 3), lax.rem(me + 2, 4), 4, 0)
     lab = jnp.stack([lab[0], lab[3], lab[1], lab[2]]).reshape(NT)
-    att1 = attend(1, meta, gather_head(ta, tb), (lab[None, :], lab[:, None]), gains, wown, wparts)
+    *att1, keep, give = attend(1, meta, (ta, tb, *others), (lab[None, :], lab[:, None], sa, sb), gains, wown, wparts)
     att1 = exchange_head(*att1)
-    sp = project(1, meta, att1, (ta, tb), out1)
-
-    near = pack(exchange_head(*fp))
-    distant = across(near, 1, 0, 0)
+    sp = project(1, meta, att1, (ta, tb, sa, sb), out1)
+
+    onward = [(w, (w + 1) % 16) for w in range(16)]
+    near = lax.ppermute(give, ("segment", "win"), onward)
+    far_keep = lax.ppermute(keep, "segment", [(1, 0)])
+    far_give = lax.ppermute(give, ("segment", "win"), [(16 + w, v) for w, v in onward])
     s_far = deliver(sp, 0, 1)
     s_local = deliver(sp, 1, 1)
-    return finish(meta, near, distant, s_far, s_local)[None]
+    return finish(meta, (near, keep), (far_give, far_keep), s_far, s_local)[None]
 
 
 def solution(mesh):

time: 262 us -> 279 us (1.065)
  the two profiles are of different devices: /device:TPU:98 before, /device:TPU:0 now
where the time goes in v1:
time: 279 us; the launch traced here: 277 us
  waiting for transfers between devices  117 us (42%)
  starting transfers between devices  78.4 us (28%)
  local copies, waits for them, and re-layouts  43.3 us (16%)
  Pallas kernels  35 us (13%)
    ppermute x9, waiting for transfers between devices, win_step(): return lax.ppermute(a, 'win', ring(16, by))  38.3 us
    ppermute x17, waiting for transfers between devices, head_step(): return lax.ppermute(a, 'head', ring(4, by))  35.1 us
    unnamed x117, local copies, waits for them, and re-layouts  33.2 us
    pallas_call x2, Pallas kernels, attend(): pl.pallas_call(functools.partial(attend_kernel, section), out_shape=out_s...  24.2 us
    ppermute x17, starting transfers between devices, head_step(): return lax.ppermute(a, 'head', ring(4, by))  17.9 us
    ppermute x1, waiting for transfers between devices, program(): gains = (gains, lax.ppermute(gains, 'segment', ring(2, 1)))  16 us
    ppermute x7, starting transfers between devices, across(): return lax.ppermute(a, ('segment', 'head'), pair_perm(source, target, by))  14.5 us
    ppermute x9, starting transfers between devices, win_step(): return lax.ppermute(a, 'win', ring(16, by))  10.6 us
  transfers between devices with their start and end apart: 57, of which 20 were waited for; matrix products, arithmetic and copies ran while one was open for 3% of the time, Pallas kernels for 10%

profile of v1, /device:TPU:0, one launch (start us, length us, event | category | flops | bytes accessed | tf_op | source)
XLA Modules:
  0.0 276.7 jit_solution(2413691349521288614)
XLA Ops:
  14.1 3.8 %collective-permute-start.21 = (bf16[4,48,1536]{2,1,0:T(8,128)(2,1)}, bf16[4,48,1536]{2,1,0:T(8,128)(2,1)}, u32[]{:S(2)}, u32[]{:S(2)}) collective-permute-start(bf16[4,48,1536]{2,1,0:T(8,128)(2,1)} %pad_maximum_fusion), channel_id=1, source_target_pairs={{0,64},{64,0},{1,65},{65,1},{2,66},{66,2},{3,67},{67,3},{4,68},{68... | collective-permute-start | bytes 1769480 | tf_op jit(solution)/shard_map/ppermute | solution.py:323
  19.7 3.5 %collective-permute-start.6 = (f32[1,1536]{1,0:T(1,128)S(1)}, f32[1,1536]{1,0:T(1,128)S(1)}, u32[]{:S(2)}, u32[]{:S(2)}) collective-permute-start(f32[1,1536]{1,0:T(1,128)S(1)} %copy-done.41), channel_id=1, source_target_pairs={{0,64},{64,0},{1,65},{65,1},{2,66},{66,2},{3,67},{67,3},{4,68},{68... | collective-permute-start | bytes 18440 | tf_op jit(solution)/shard_map/ppermute | solution.py:320
  23.2 16.0 %collective-permute-done.6.refs_11_.refs_14_ = f32[1,1536]{1,0:T(1,128)S(1)} collective-permute-done((f32[1,1536]{1,0:T(1,128)S(1)}, f32[1,1536]{1,0:T(1,128)S(1)}, u32[]{:S(2)}, u32[]{:S(2)}) %collective-permute-start.6) | collective-permute-done | bytes 6176 | tf_op jit(solution)/shard_map/ppermute | solution.py:320
  43.5 4.9 %collective-permute-done.1.refs_4_ = bf16[480,384]{1,0:T(8,128)(2,1)S(1)} collective-permute-done((bf16[480,384]{1,0:T(8,128)(2,1)S(1)}, bf16[480,384]{1,0:T(8,128)(2,1)S(1)}, u32[]{:S(2)}, u32[]{:S(2)}) %collective-permute-start.1) | collective-permute-done | bytes 368672 | tf_op jit(solution)/shard_map/ppermute | solution.py:32
  62.3 7.4 %collective-permute-done.9.refs_15_.refs_18_ = bf16[3,192,384]{2,1,0:T(8,128)(2,1)S(1)} collective-permute-done((bf16[3,192,384]{2,1,0:T(8,128)(2,1)S(1)}, bf16[3,192,384]{2,1,0:T(8,128)(2,1)S(1)}, u32[]{:S(2)}, u32[]{:S(2)}) %collective-permute-start.9) | collective-permute-done | bytes 442400 | tf_op jit(solution)/shard_map/ppermute | solution.py:231
  70.5 3.8 %collective-permute-done.10.refs_16_.refs_19_ = bf16[3,192,384]{2,1,0:T(8,128)(2,1)} collective-permute-done((bf16[3,192,384]{2,1,0:T(8,128)(2,1)S(1)}, bf16[3,192,384]{2,1,0:T(8,128)(2,1)}, u32[]{:S(2)}, u32[]{:S(2)}) %collective-permute-start.10) | collective-permute-done | bytes 442400 | tf_op jit(solution)/shard_map/ppermute | solution.py:231
  77.1 8.7 %collective-permute-done.22.refs_7_ = bf16[4,48,1536]{2,1,0:T(8,128)(2,1)} collective-permute-done((bf16[4,48,1536]{2,1,0:T(8,128)(2,1)S(1)}, bf16[4,48,1536]{2,1,0:T(8,128)(2,1)}, u32[]{:S(2)}, u32[]{:S(2)}) %collective-permute-start.22) | collective-permute-done | bytes 589856 | tf_op jit(solution)/shard_map/ppermute | solution.py:231
  94.9 12.5 %shard_map.55 = (bf16[240,384]{1,0:T(8,128)(2,1)S(1)}, bf16[240,384]{1,0:T(8,128)(2,1)S(1)}, bf16[240,384]{1,0:T(8,128)(2,1)S(1)}, bf16[240,384]{1,0:T(8,128)(2,1)S(1)}, bf16[240,1536]{1,0:T(8,128)(2,1)S(1)}) custom-call(s32[4]{0:T(128)S(1)} %pad_add_fusion.refs_0_.meta_ref, bf16[480,384]{1,0:T(8,128)(2,1)S(1)} %copy-done.16, ...), custom_call_target="tpu_custom_call" | custom-call | tf_op jit(solution)/shard_map/pallas_call | solution.py:164
  111.2 4.7 %collective-permute-done.15.refs_1_ = bf16[240,384]{1,0:T(8,128)(2,1)S(1)} collective-permute-done((bf16[240,384]{1,0:T(8,128)(2,1)S(1)}, bf16[240,384]{1,0:T(8,128)(2,1)S(1)}, u32[]{:S(2)}, u32[]{:S(2)}) %collective-permute-start.15) | collective-permute-done | bytes 184352 | tf_op jit(solution)/shard_map/ppermute | solution.py:32
  122.3 3.5 %shard_map.56 = (bf16[120,1536]{1,0:T(8,128)(2,1)S(1)}, bf16[120,1536]{1,0:T(8,128)(2,1)S(1)}) custom-call(s32[4]{0:T(128)S(1)} %pad_add_fusion.refs_0_.meta_ref, bf16[240,384]{1,0:T(8,128)(2,1)S(1)} %get-tuple-element.22.refs_0_, bf16[240,384]{1,0:T(8,128)(2,1)S(1)} %collective-permute-done.15.refs_1_, ...), custom_call_target="tpu_custom_call" | custom-call | tf_op jit(solution)/shard_map/pallas_call | solution.py:204
  129.7 17.7 %collective-permute-done.43.refs_9_ = bf16[4,48,1536]{2,1,0:T(8,128)(2,1)} collective-permute-done((bf16[4,48,1536]{2,1,0:T(8,128)(2,1)S(1)}, bf16[4,48,1536]{2,1,0:T(8,128)(2,1)}, u32[]{:S(2)}, u32[]{:S(2)}) %collective-permute-start.43) | collective-permute-done | bytes 589856 | tf_op jit(solution)/shard_map/ppermute | solution.py:231
  147.4 8.3 %collective-permute-start.35 = (bf16[120,1536]{1,0:T(8,128)(2,1)S(1)}, bf16[120,1536]{1,0:T(8,128)(2,1)S(1)}, u32[]{:S(2)}, u32[]{:S(2)}) collective-permute-start(bf16[120,1536]{1,0:T(8,128)(2,1)S(1)} %get-tuple-element.27.refs_1_.refs_4_), channel_id=1, source_target_pairs={{4,0},{5,1},{8,4},{9,5},{12,8},{13,9},{16,12},{17,13},{20,16},{21,... | collective-permute-start | bytes 1105928 | tf_op jit(solution)/shard_map/ppermute | solution.py:345
  160.7 4.6 %collective-permute-start.46 = (bf16[4,48,1536]{2,1,0:T(8,128)(2,1)S(1)}, bf16[4,48,1536]{2,1,0:T(8,128)(2,1)}, u32[]{:S(2)}, u32[]{:S(2)}) collective-permute-start(bf16[4,48,1536]{2,1,0:T(8,128)(2,1)S(1)} %get-tuple-element.39.refs_8_), channel_id=1, source_target_pairs={{0,4},{4,0},{8,12},{12,8},{16,20},{20,16},{24,28},{28,24},{32,36},... | collective-permute-start | bytes 1769480 | tf_op jit(solution)/shard_map/ppermute | solution.py:240
  173.6 9.9 %collective-permute-done.34.refs_8_ = bf16[120,1536]{1,0:T(8,128)(2,1)} collective-permute-done((bf16[120,1536]{1,0:T(8,128)(2,1)}, bf16[120,1536]{1,0:T(8,128)(2,1)}, u32[]{:S(2)}, u32[]{:S(2)}) %collective-permute-start.34) | collective-permute-done | bytes 368672 | tf_op jit(solution)/shard_map/ppermute | solution.py:32
  195.5 11.7 %shard_map.57 = (bf16[240,384]{1,0:T(8,128)(2,1)S(1)}, bf16[240,384]{1,0:T(8,128)(2,1)S(1)}, bf16[240,384]{1,0:T(8,128)(2,1)S(1)}, bf16[240,384]{1,0:T(8,128)(2,...) custom-call(s32[4]{0:T(128)S(1)} %pad_add_fusion.refs_0_.meta_ref, ...), custom_call_target="tpu_custom_call" | custom-call | tf_op jit(solution)/shard_map/pallas_call | solution.py:164
  210.5 4.6 %collective-permute-done.40.refs_1_ = bf16[240,384]{1,0:T(8,128)(2,1)S(1)} collective-permute-done((bf16[240,384]{1,0:T(8,128)(2,1)S(1)}, bf16[240,384]{1,0:T(8,128)(2,1)S(1)}, u32[]{:S(2)}, u32[]{:S(2)}) %collective-permute-start.40) | collective-permute-done | bytes 184352 | tf_op jit(solution)/shard_map/ppermute | solution.py:32
  218.1 3.9 %shard_map.58 = (bf16[240,384]{1,0:T(8,128)(2,1)S(1)}, bf16[240,384]{1,0:T(8,128)(2,1)S(1)}, bf16[240,384]{1,0:T(8,128)(2,1)S(1)}, bf16[240,384]{1,0:T(8,128)(2,1)S(1)}) custom-call(s32[4]{0:T(128)S(1)} %pad_add_fusion.refs_0_.meta_ref, bf16[240,384]{1,0:T(8,128)(2,1)S(1)} %get-tuple-element.31.refs_0_, ...), custom_call_target="tpu_custom_call" | custom-call | tf_op jit(solution)/shard_map/pallas_call | solution.py:204
  222.0 6.2 %collective-permute-start.50 = (bf16[240,384]{1,0:T(8,128)(2,1)S(1)}, bf16[240,384]{1,0:T(8,128)(2,1)S(1)}, u32[]{:S(2)}, u32[]{:S(2)}) collective-permute-start(bf16[240,384]{1,0:T(8,128)(2,1)S(1)} %get-tuple-element.35.refs_8_), channel_id=1, source_target_pairs={{0,64},{1,65},{2,66},{3,67},{4,68},{5,69},{6,70},{7,71},{8,72},{9,... | collective-permute-start | bytes 552968 | tf_op jit(solution)/shard_map/ppermute | solution.py:296
  229.8 3.4 %collective-permute-start.52 = (bf16[240,384]{1,0:T(8,128)(2,1)S(1)}, bf16[240,384]{1,0:T(8,128)(2,1)S(1)}, u32[]{:S(2)}, u32[]{:S(2)}) collective-permute-start(bf16[240,384]{1,0:T(8,128)(2,1)S(1)} %get-tuple-element.37), channel_id=1, source_target_pairs={{0,67},{1,64},{2,65},{3,66},{4,71},{5,68},{6,69},{7,70},{8,75},{9,... | collective-permute-start | bytes 552968 | tf_op jit(solution)/shard_map/ppermute | solution.py:296
  236.5 7.4 %collective-permute-done.50.refs_4_ = bf16[240,384]{1,0:T(8,128)(2,1)S(1)} collective-permute-done((bf16[240,384]{1,0:T(8,128)(2,1)S(1)}, bf16[240,384]{1,0:T(8,128)(2,1)S(1)}, u32[]{:S(2)}, u32[]{:S(2)}) %collective-permute-start.50) | collective-permute-done | bytes 184352 | tf_op jit(solution)/shard_map/ppermute | solution.py:296
  248.6 9.7 %collective-permute-done.38.refs_2_ = bf16[2,240,384]{2,1,0:T(8,128)(2,1)S(1)} collective-permute-done((bf16[2,240,384]{2,1,0:T(8,128)(2,1)S(1)}, bf16[2,240,384]{2,1,0:T(8,128)(2,1)S(1)}, u32[]{:S(2)}, u32[]{:S(2)}) %collective-permute-start.38) | collective-permute-done | bytes 368672 | tf_op jit(solution)/shard_map/ppermute | solution.py:357
  258.3 10.2 %collective-permute-done.39.refs_3_ = bf16[2,240,384]{2,1,0:T(8,128)(2,1)S(1)} collective-permute-done((bf16[2,240,384]{2,1,0:T(8,128)(2,1)S(1)}, bf16[2,240,384]{2,1,0:T(8,128)(2,1)S(1)}, u32[]{:S(2)}, u32[]{:S(2)}) %collective-permute-start.39) | collective-permute-done | bytes 368672 | tf_op jit(solution)/shard_map/ppermute | solution.py:356
  269.3 3.5 %finish.1 = bf16[2,30,30,384]{3,2,1,0:T(8,128)(2,1)} custom-call(s32[4]{0:T(128)} %copy-done.42, bf16[2,240,384]{2,1,0:T(8,128)(2,1)} %copy-done.47, bf16[2,240,384]{2,1,0:T(8,128)(2,1)} %copy-done.31, bf16[2,240,384]{2,1,0:T(8,128)(2,1)} %copy-done.48, bf16[2,240,384]{2,1,0:T(8,128)(2,1)} %copy-done.49, bf16[240,384]{1,0:T(8,128)(2,1)} %copy-done.50, ...), custom_call_target="tpu_custom_call" | custom-call | tf_op jit(solution)/shard_map/finish/pallas_call | solution.py:281
  272.8 3.9 %copy.9 = bf16[1,2,30,30,384]{4,1,3,2,0:T(2,128)(2,1)} copy(bf16[1,2,30,30,384]{4,3,2,1,0:T(8,128)(2,1)} %bitcast.26) | data formatting | bytes 2764800 | tf_op jit(solution)/shard_map/broadcast_in_dim | solution.py:360
  (241 shorter events, 102.2 us)
Async XLA Ops:
  8.0 32.0 %collective-permute-start.3 = (bf16[480,384]{1,0:T(8,128)(2,1)S(1)}, bf16[480,384]{1,0:T(8,128)(2,1)S(1)}, u32[]{:S(2)}, u32[]{:S(2)}) collective-permute-start(bf16[480,384]{1,0:T(8,128)(2,1)S(1)} %fusion.5.refs_2_), channel_id=1, source_target_pairs={{0,3},{1,0},{2,1},{3,2},{4,7},{5,4},{6,5},{7,6},{8,11},{9,8},{10,9... | collective-permute-start | bytes 1105928 | tf_op jit(solution)/shard_map/ppermute | solution.py:32
  9.3 33.2 %collective-permute-start = (bf16[480,384]{1,0:T(8,128)(2,1)S(1)}, bf16[480,384]{1,0:T(8,128)(2,1)}, u32[]{:S(2)}, u32[]{:S(2)}) collective-permute-start(bf16[480,384]{1,0:T(8,128)(2,1)S(1)} %fusion.3.refs_1_), channel_id=1, source_target_pairs={{0,1},{1,2},{2,3},{3,0},{4,5},{5,6},{6,7},{7,4},{8,9},{9,10},{10,1... | collective-permute-start | bytes 1105928 | tf_op jit(solution)/shard_map/ppermute | solution.py:32
  14.1 44.7 %collective-permute-start.21 = (bf16[4,48,1536]{2,1,0:T(8,128)(2,1)}, bf16[4,48,1536]{2,1,0:T(8,128)(2,1)}, u32[]{:S(2)}, u32[]{:S(2)}) collective-permute-start(bf16[4,48,1536]{2,1,0:T(8,128)(2,1)} %pad_maximum_fusion), channel_id=1, source_target_pairs={{0,64},{64,0},{1,65},{65,1},{2,66},{66,2},{3,67},{67,3},{4,68},{68... | collective-permute-start | bytes 1769480 | tf_op jit(solution)/shard_map/ppermute | solution.py:323
  19.7 29.5 %collective-permute-start.7 = (bf16[3,192,384]{2,1,0:T(8,128)(2,1)}, bf16[3,192,384]{2,1,0:T(8,128)(2,1)S(1)}, u32[]{:S(2)}, u32[]{:S(2)}) collective-permute-start(bf16[3,192,384]{2,1,0:T(8,128)(2,1)} %dynamic-slice_bitcast_fusion), channel_id=1, source_target_pairs={{0,64},{64,0},{1,65},{65,1},{2,66},{66,2},{3,67},{67,3},{4,68},{68... | collective-permute-start | bytes 1327112 | tf_op jit(solution)/shard_map/ppermute | solution.py:318
  19.7 19.5 %collective-permute-start.6 = (f32[1,1536]{1,0:T(1,128)S(1)}, f32[1,1536]{1,0:T(1,128)S(1)}, u32[]{:S(2)}, u32[]{:S(2)}) collective-permute-start(f32[1,1536]{1,0:T(1,128)S(1)} %copy-done.41), channel_id=1, source_target_pairs={{0,64},{64,0},{1,65},{65,1},{2,66},{66,2},{3,67},{67,3},{4,68},{68... | collective-permute-start | bytes 18440 | tf_op jit(solution)/shard_map/ppermute | solution.py:320
  51.4 18.2 %collective-permute-start.9 = (bf16[3,192,384]{2,1,0:T(8,128)(2,1)S(1)}, bf16[3,192,384]{2,1,0:T(8,128)(2,1)S(1)}, u32[]{:S(2)}, u32[]{:S(2)}) collective-permute-start(bf16[3,192,384]{2,1,0:T(8,128)(2,1)S(1)} %collective-permute-done.7.refs_13_.refs_16_), channel_id=1, source_target_pairs={{0,48},{4,52},{8,56},{12,60},{16,0},{20,4},{24,8},{28,12},{32,16},... | collective-permute-start | bytes 1327112 | tf_op jit(solution)/shard_map/ppermute | solution.py:231
  55.6 18.6 %collective-permute-start.10 = (bf16[3,192,384]{2,1,0:T(8,128)(2,1)S(1)}, bf16[3,192,384]{2,1,0:T(8,128)(2,1)}, u32[]{:S(2)}, u32[]{:S(2)}) collective-permute-start(bf16[3,192,384]{2,1,0:T(8,128)(2,1)S(1)} %collective-permute-done.7.refs_13_.refs_16_), channel_id=1, source_target_pairs={{0,32},{4,36},{8,40},{12,44},{16,48},{20,52},{24,56},{28,60},{32,0... | collective-permute-start | bytes 1327112 | tf_op jit(solution)/shard_map/ppermute | solution.py:231
  61.0 24.8 %collective-permute-start.22 = (bf16[4,48,1536]{2,1,0:T(8,128)(2,1)S(1)}, bf16[4,48,1536]{2,1,0:T(8,128)(2,1)}, u32[]{:S(2)}, u32[]{:S(2)}) collective-permute-start(bf16[4,48,1536]{2,1,0:T(8,128)(2,1)S(1)} %get-tuple-element.40.refs_6_), channel_id=1, source_target_pairs={{0,16},{4,20},{8,24},{12,28},{16,32},{20,36},{24,40},{28,44},{32,4... | collective-permute-start | bytes 1769480 | tf_op jit(solution)/shard_map/ppermute | solution.py:231
  74.2 33.3 %collective-permute-start.23 = (bf16[4,48,1536]{2,1,0:T(8,128)(2,1)S(1)}, bf16[4,48,1536]{2,1,0:T(8,128)(2,1)}, u32[]{:S(2)}, u32[]{:S(2)}) collective-permute-start(bf16[4,48,1536]{2,1,0:T(8,128)(2,1)S(1)} %get-tuple-element.40.refs_6_), channel_id=1, source_target_pairs={{0,48},{4,52},{8,56},{12,60},{16,0},{20,4},{24,8},{28,12},{32,16},... | collective-permute-start | bytes 1769480 | tf_op jit(solution)/shard_map/ppermute | solution.py:231
  75.0 35.7 %collective-permute-start.24 = (bf16[4,48,1536]{2,1,0:T(8,128)(2,1)S(1)}, bf16[4,48,1536]{2,1,0:T(8,128)(2,1)}, u32[]{:S(2)}, u32[]{:S(2)}) collective-permute-start(bf16[4,48,1536]{2,1,0:T(8,128)(2,1)S(1)} %get-tuple-element.40.refs_6_), channel_id=1, source_target_pairs={{0,32},{4,36},{8,40},{12,44},{16,48},{20,52},{24,56},{28,60},{32,0... | collective-permute-start | bytes 1769480 | tf_op jit(solution)/shard_map/ppermute | solution.py:231
  76.7 34.4 %collective-permute-start.25 = (bf16[4,48,1536]{2,1,0:T(8,128)(2,1)S(1)}, bf16[4,48,1536]{2,1,0:T(8,128)(2,1)}, u32[]{:S(2)}, u32[]{:S(2)}) collective-permute-start(bf16[4,48,1536]{2,1,0:T(8,128)(2,1)S(1)} %get-tuple-element.40.refs_6_), channel_id=1, source_target_pairs={{0,4},{4,0},{8,12},{12,8},{16,20},{20,16},{24,28},{28,24},{32,36},... | collective-permute-start | bytes 1769480 | tf_op jit(solution)/shard_map/ppermute | solution.py:240
  85.8 36.4 %collective-permute-start.26 = (bf16[4,48,1536]{2,1,0:T(8,128)(2,1)}, bf16[4,48,1536]{2,1,0:T(8,128)(2,1)}, u32[]{:S(2)}, u32[]{:S(2)}) collective-permute-start(bf16[4,48,1536]{2,1,0:T(8,128)(2,1)} %collective-permute-done.22.refs_7_), channel_id=1, source_target_pairs={{0,4},{4,0},{8,12},{12,8},{16,20},{20,16},{24,28},{28,24},{32,36},... | collective-permute-start | bytes 1769480 | tf_op jit(solution)/shard_map/ppermute | solution.py:240
  119.0 28.4 %collective-permute-start.43 = (bf16[4,48,1536]{2,1,0:T(8,128)(2,1)S(1)}, bf16[4,48,1536]{2,1,0:T(8,128)(2,1)}, u32[]{:S(2)}, u32[]{:S(2)}) collective-permute-start(bf16[4,48,1536]{2,1,0:T(8,128)(2,1)S(1)} %get-tuple-element.39.refs_8_), channel_id=1, source_target_pairs={{0,16},{4,20},{8,24},{12,28},{16,32},{20,36},{24,40},{28,44},{32,4... | collective-permute-start | bytes 1769480 | tf_op jit(solution)/shard_map/ppermute | solution.py:231
  120.0 27.3 %collective-permute-start.44 = (bf16[4,48,1536]{2,1,0:T(8,128)(2,1)S(1)}, bf16[4,48,1536]{2,1,0:T(8,128)(2,1)}, u32[]{:S(2)}, u32[]{:S(2)}) collective-permute-start(bf16[4,48,1536]{2,1,0:T(8,128)(2,1)S(1)} %get-tuple-element.39.refs_8_), channel_id=1, source_target_pairs={{0,48},{4,52},{8,56},{12,60},{16,0},{20,4},{24,8},{28,12},{32,16},... | collective-permute-start | bytes 1769480 | tf_op jit(solution)/shard_map/ppermute | solution.py:231
  122.2 25.2 %collective-permute-start.45 = (bf16[4,48,1536]{2,1,0:T(8,128)(2,1)S(1)}, bf16[4,48,1536]{2,1,0:T(8,128)(2,1)}, u32[]{:S(2)}, u32[]{:S(2)}) collective-permute-start(bf16[4,48,1536]{2,1,0:T(8,128)(2,1)S(1)} %get-tuple-element.39.refs_8_), channel_id=1, source_target_pairs={{0,32},{4,36},{8,40},{12,44},{16,48},{20,52},{24,56},{28,60},{32,0... | collective-permute-start | bytes 1769480 | tf_op jit(solution)/shard_map/ppermute | solution.py:231
  125.8 30.7 %collective-permute-start.29 = (bf16[120,1536]{1,0:T(8,128)(2,1)S(1)}, bf16[120,1536]{1,0:T(8,128)(2,1)S(1)}, u32[]{:S(2)}, u32[]{:S(2)}) collective-permute-start(bf16[120,1536]{1,0:T(8,128)(2,1)S(1)} %get-tuple-element.27.refs_1_.refs_4_), channel_id=1, source_target_pairs={{4,1},{5,2},{2,3},{3,0},{8,5},{9,6},{6,7},{7,4},{12,9},{13,10},{10... | collective-permute-start | bytes 1105928 | tf_op jit(solution)/shard_map/ppermute | solution.py:341
  127.6 31.6 %collective-permute-start.32 = (bf16[120,1536]{1,0:T(8,128)(2,1)S(1)}, bf16[120,1536]{1,0:T(8,128)(2,1)}, u32[]{:S(2)}, u32[]{:S(2)}) collective-permute-start(bf16[120,1536]{1,0:T(8,128)(2,1)S(1)} %get-tuple-element.28.refs_2_.refs_5_), channel_id=1, source_target_pairs={{4,3},{5,0},{2,1},{3,2},{8,7},{9,4},{6,5},{7,6},{12,11},{13,8},{10... | collective-permute-start | bytes 1105928 | tf_op jit(solution)/shard_map/ppermute | solution.py:341
  147.4 18.7 %collective-permute-start.35 = (bf16[120,1536]{1,0:T(8,128)(2,1)S(1)}, bf16[120,1536]{1,0:T(8,128)(2,1)S(1)}, u32[]{:S(2)}, u32[]{:S(2)}) collective-permute-start(bf16[120,1536]{1,0:T(8,128)(2,1)S(1)} %get-tuple-element.27.refs_1_.refs_4_), channel_id=1, source_target_pairs={{4,0},{5,1},{8,4},{9,5},{12,8},{13,9},{16,12},{17,13},{20,16},{21,... | collective-permute-start | bytes 1105928 | tf_op jit(solution)/shard_map/ppermute | solution.py:345
  160.7 46.6 %collective-permute-start.46 = (bf16[4,48,1536]{2,1,0:T(8,128)(2,1)S(1)}, bf16[4,48,1536]{2,1,0:T(8,128)(2,1)}, u32[]{:S(2)}, u32[]{:S(2)}) collective-permute-start(bf16[4,48,1536]{2,1,0:T(8,128)(2,1)S(1)} %get-tuple-element.39.refs_8_), channel_id=1, source_target_pairs={{0,4},{4,0},{8,12},{12,8},{16,20},{20,16},{24,28},{28,24},{32,36},... | collective-permute-start | bytes 1769480 | tf_op jit(solution)/shard_map/ppermute | solution.py:240
  166.0 44.5 %collective-permute-start.47 = (bf16[4,48,1536]{2,1,0:T(8,128)(2,1)}, bf16[4,48,1536]{2,1,0:T(8,128)(2,1)}, u32[]{:S(2)}, u32[]{:S(2)}) collective-permute-start(bf16[4,48,1536]{2,1,0:T(8,128)(2,1)} %collective-permute-done.43.refs_9_), channel_id=1, source_target_pairs={{0,4},{4,0},{8,12},{12,8},{16,20},{20,16},{24,28},{28,24},{32,36},... | collective-permute-start | bytes 1769480 | tf_op jit(solution)/shard_map/ppermute | solution.py:240
  166.9 43.6 %collective-permute-start.48 = (bf16[4,48,1536]{2,1,0:T(8,128)(2,1)}, bf16[4,48,1536]{2,1,0:T(8,128)(2,1)}, u32[]{:S(2)}, u32[]{:S(2)}) collective-permute-start(bf16[4,48,1536]{2,1,0:T(8,128)(2,1)} %collective-permute-done.44.refs_10_), channel_id=1, source_target_pairs={{0,4},{4,0},{8,12},{12,8},{16,20},{20,16},{24,28},{28,24},{32,36},... | collective-permute-start | bytes 1769480 | tf_op jit(solution)/shard_map/ppermute | solution.py:240
  169.0 41.5 %collective-permute-start.49 = (bf16[4,48,1536]{2,1,0:T(8,128)(2,1)}, bf16[4,48,1536]{2,1,0:T(8,128)(2,1)}, u32[]{:S(2)}, u32[]{:S(2)}) collective-permute-start(bf16[4,48,1536]{2,1,0:T(8,128)(2,1)} %collective-permute-done.45.refs_11_), channel_id=1, source_target_pairs={{0,4},{4,0},{8,12},{12,8},{16,20},{20,16},{24,28},{28,24},{32,36},... | collective-permute-start | bytes 1769480 | tf_op jit(solution)/shard_map/ppermute | solution.py:240
  222.0 21.8 %collective-permute-start.50 = (bf16[240,384]{1,0:T(8,128)(2,1)S(1)}, bf16[240,384]{1,0:T(8,128)(2,1)S(1)}, u32[]{:S(2)}, u32[]{:S(2)}) collective-permute-start(bf16[240,384]{1,0:T(8,128)(2,1)S(1)} %get-tuple-element.35.refs_8_), channel_id=1, source_target_pairs={{0,64},{1,65},{2,66},{3,67},{4,68},{5,69},{6,70},{7,71},{8,72},{9,... | collective-permute-start | bytes 552968 | tf_op jit(solution)/shard_map/ppermute | solution.py:296
  245.9 22.7 %collective-permute-start.39 = (bf16[2,240,384]{2,1,0:T(8,128)(2,1)S(1)}, bf16[2,240,384]{2,1,0:T(8,128)(2,1)S(1)}, u32[]{:S(2)}, u32[]{:S(2)}) collective-permute-start(bf16[2,240,384]{2,1,0:T(8,128)(2,1)S(1)} %get-tuple-element.30.refs_1_), channel_id=1, source_target_pairs={{64,0},{65,1},{66,2},{67,3},{68,4},{69,5},{70,6},{71,7},{72,8},{73... | collective-permute-start | bytes 1105928 | tf_op jit(solution)/shard_map/ppermute | solution.py:356
  (91 other events, 921.1 us)

commit v2 on v1

--- a/solution.py
+++ b/solution.py
@@ -43,7 +43,7 @@
 
 def attend_kernel(section, *refs):
     meta_ref, xparts = refs[0], refs[1:9]
-    masks, refs = (refs[9:10], refs[10:]) if section == 0 else (refs[9:13], refs[13:])
+    masks, refs = (refs[9:10], refs[10:]) if section == 0 else (refs[9:11], refs[11:])
     gain_ref, other_gain_ref, wown, wparts, outs, refs = refs[0], refs[1], refs[2], refs[3:11], refs[11:15], refs[15:]
     if section == 0:
         v_ref, xs, q_s, k_s, u_s, w_s, s_s, a_s, sem = refs
@@ -76,12 +76,6 @@
     if section == 1:
         for i in range(8):
             xs[i * HALF : (i + 1) * HALF, :] = xparts[i][...]
-
-        @pl.when(me < 2)
-        def _():
-            for i in range(2):
-                xs[i * HALF : (i + 1) * HALF, :] = masks[2 + i][...]
-
         lanes = pl.ds(pl.multiple_of(me * FQ, FQ), FQ)
         for r in range(4):
             g_s[lax.rem(me + REL[r], 4)] = xs[r * TS : (r + 1) * TS, lanes]
@@ -172,9 +166,8 @@
 
 
 def project_kernel(section, meta_ref, *refs):
-    n = 6 if section == 0 else 8
-    att, vparts, wparts = refs[:4], refs[4:n], refs[n : n + 8]
-    outs, (w_s, a_s, t_s) = refs[n + 8 : -3], refs[-3:]
+    att, vparts, wparts = refs[:4], refs[4:6], refs[6:14]
+    outs, (w_s, a_s, t_s) = refs[14:-3], refs[-3:]
     me = meta_ref[1]
     for block, ref in zip(set_rows(meta_ref), wparts):
         for r in range(4):
@@ -184,10 +177,7 @@
     acc = jnp.dot(a_s[...], w_s[...], preferred_element_type=F32)
     for i in range(2):
         rows = slice(i * HALF, (i + 1) * HALF)
-        v = vparts[i][...].astype(F32)
-        if section == 1:
-            v = jnp.where(me < 2, vparts[2 + i][...].astype(F32), v)
-        t_s[rows, :] = (acc[rows, :] + v).astype(BF16)
+        t_s[rows, :] = (acc[rows, :] + vparts[i][...].astype(F32)).astype(BF16)
         if section == 0:
             outs[i][...] = t_s[rows, :]
     if section == 1:
@@ -204,7 +194,7 @@
     return pl.pallas_call(
         functools.partial(project_kernel, section),
         out_shape=out_shape,
-        in_specs=[SM] + [VM] * (12 + len(vparts)),
+        in_specs=[SM] + [VM] * 14,
         out_specs=[VM] * len(out_shape),
         scratch_shapes=[pltpu.VMEM((D, D), BF16), pltpu.VMEM((TS, D), BF16), pltpu.VMEM((TS, D), BF16)],
         compiler_params=pltpu.CompilerParams(vmem_limit_bytes=20 << 20),
@@ -342,14 +332,14 @@
 
     others = gather_head(ta, tb, shifted_step)
     perm = [(source(w, i), w * 4 + i) for w in range(16) for i in (0, 1)]
-    sa = lax.ppermute(ta, ("win", "head"), perm)
-    sb = lax.ppermute(tb, ("win", "head"), perm)
+    ta = jnp.where(me < 2, lax.ppermute(ta, ("win", "head"), perm), ta)
+    tb = jnp.where(me < 2, lax.ppermute(tb, ("win", "head"), perm), tb)
     lab = jnp.stack(slot_groups(labels.astype(F32), -1.0)).reshape(4, TS)
     lab = lax.dynamic_slice_in_dim(jnp.concatenate([lab] * 3), lax.rem(me + 2, 4), 4, 0)
     lab = jnp.stack([lab[0], lab[3], lab[1], lab[2]]).reshape(NT)
-    *att1, keep, give = attend(1, meta, (ta, tb, *others), (lab[None, :], lab[:, None], sa, sb), gains, wown, wparts)
+    *att1, keep, give = attend(1, meta, (ta, tb, *others), (lab[None, :], lab[:, None]), gains, wown, wparts)
     att1 = exchange_head(*att1)
-    sp = project(1, meta, att1, (ta, tb, sa, sb), out1)
+    sp = project(1, meta, att1, (ta, tb), out1)
 
     onward = [(w, (w + 1) % 16) for w in range(16)]
     near = lax.ppermute(give, ("segment", "win"), onward)

time: 279 us -> 259 us (0.928)
  starting transfers between devices: 78.4 us -> 60.4 us
  local copies, waits for them, and re-layouts: 43.3 us -> 26.8 us
  waiting for transfers between devices: 117 us -> 131 us
    unnamed x117 -> x89, local copies, waits for them, and re-layouts: 33.2 us -> 16.7 us
    ppermute x17, waiting for transfers between devices: 35.1 us -> 48.5 us  [head_step(): return lax.ppermute(a, 'head', ring(4, by))]
    ppermute x1, waiting for transfers between devices: 16 us -> 4.23 us  [program(): gains = (gains, lax.ppermute(gains, 'segment', ring(2, 1)))]
    ppermute x4, waiting for transfers between devices: 0.01 us -> 9.58 us  [shifted_step(): return lax.ppermute(part, ('win', 'head'), perm)]
    ppermute x12, starting transfers between devices: 9.42 us -> 1.77 us  [gather_win(): swapped.append(lax.ppermute(a, 'win', [(j, j ^ 1) for j in range(16)]))]
    ppermute x7, starting transfers between devices: 14.5 us -> 7.87 us  [across(): return lax.ppermute(a, ('segment', 'head'), pair_perm(source, target, by))]
    ppermute x2, starting transfers between devices: 10.2 us -> 3.82 us  [the longest x1 1.91 us: program(): tb = jnp.where(me < 2, lax.ppermute(tb, ('win', 'head'), perm), tb)]
    ppermute x9, waiting for transfers between devices: 38.3 us -> 32.3 us  [win_step(): return lax.ppermute(a, 'win', ring(16, by))]
  transfers between devices with their start and end apart: 57 -> 57, of which waited for: 20 -> 24; matrix products, arithmetic and copies ran while one was open for 3% -> 4% of each run, Pallas kernels for 10% -> 11%
where the time goes in v2:
time: 259 us; the launch traced here: 258 us
  waiting for transfers between devices  131 us (51%)
  starting transfers between devices  60.4 us (23%)
  Pallas kernels  34.7 us (13%)
  local copies, waits for them, and re-layouts  26.8 us (10%)
  other arithmetic  4.55 us (2%)
    ppermute x17, waiting for transfers between devices, head_step(): return lax.ppermute(a, 'head', ring(4, by))  48.5 us
    ppermute x9, waiting for transfers between devices, win_step(): return lax.ppermute(a, 'win', ring(16, by))  32.3 us
    pallas_call x2, Pallas kernels, attend(): pl.pallas_call(functools.partial(attend_kernel, section), out_shape=out_s...  24.3 us
    ppermute x17, starting transfers between devices, head_step(): return lax.ppermute(a, 'head', ring(4, by))  18.2 us
    unnamed x89, local copies, waits for them, and re-layouts  16.7 us
    ppermute x9, starting transfers between devices, win_step(): return lax.ppermute(a, 'win', ring(16, by))  11.4 us
    ppermute x7, waiting for transfers between devices, across(): return lax.ppermute(a, ('segment', 'head'), pair_perm(source, target, by))  9.94 us
    ppermute x1, waiting for transfers between devices, program(): lax.ppermute(give, ('segment', 'win'), [(16 + w, v) for w, v in onward])  9.85 us
  transfers between devices with their start and end apart: 57, of which 24 were waited for; matrix products, arithmetic and copies ran while one was open for 4% of the time, Pallas kernels for 11%

profile of v2, /device:TPU:0, one launch (start us, length us, event | category | flops | bytes accessed | tf_op | source)
XLA Modules:
  0.0 258.1 jit_solution(145475204206245687)
XLA Ops:
  8.1 3.9 %collective-permute-start.7 = (bf16[3,192,384]{2,1,0:T(8,128)(2,1)}, bf16[3,192,384]{2,1,0:T(8,128)(2,1)S(1)}, u32[]{:S(2)}, u32[]{:S(2)}) collective-permute-start(bf16[3,192,384]{2,1,0:T(8,128)(2,1)} %dynamic-slice_bitcast_fusion), channel_id=1, source_target_pairs={{0,64},{64,0},{1,65},{65,1},{2,66},{66,2},{3,67},{67,3},{4,68},{68... | collective-permute-start | bytes 1327112 | tf_op jit(solution)/shard_map/ppermute | solution.py:308
  18.5 4.2 %collective-permute-done.6.refs_11_.refs_12_ = f32[1,1536]{1,0:T(1,128)S(1)} collective-permute-done((f32[1,1536]{1,0:T(1,128)S(1)}, f32[1,1536]{1,0:T(1,128)S(1)}, u32[]{:S(2)}, u32[]{:S(2)}) %collective-permute-start.6) | collective-permute-done | bytes 6176 | tf_op jit(solution)/shard_map/ppermute | solution.py:310
  28.2 5.9 %collective-permute-done.refs_3_ = bf16[480,384]{1,0:T(8,128)(2,1)S(1)} collective-permute-done((bf16[480,384]{1,0:T(8,128)(2,1)S(1)}, bf16[480,384]{1,0:T(8,128)(2,1)S(1)}, u32[]{:S(2)}, u32[]{:S(2)}) %collective-permute-start) | collective-permute-done | bytes 368672 | tf_op jit(solution)/shard_map/ppermute | solution.py:32
  36.5 9.2 %collective-permute-done.2.refs_5_ = bf16[480,384]{1,0:T(8,128)(2,1)} collective-permute-done((bf16[480,384]{1,0:T(8,128)(2,1)S(1)}, bf16[480,384]{1,0:T(8,128)(2,1)}, u32[]{:S(2)}, u32[]{:S(2)}) %collective-permute-start.2) | collective-permute-done | bytes 368672 | tf_op jit(solution)/shard_map/ppermute | solution.py:32
  45.7 4.6 %collective-permute-done.5.refs_8_ = bf16[480,384]{1,0:T(8,128)(2,1)} collective-permute-done((bf16[480,384]{1,0:T(8,128)(2,1)S(1)}, bf16[480,384]{1,0:T(8,128)(2,1)}, u32[]{:S(2)}, u32[]{:S(2)}) %collective-permute-start.5) | collective-permute-done | bytes 368672 | tf_op jit(solution)/shard_map/ppermute | solution.py:32
  50.3 3.2 %collective-permute-start.10 = (bf16[3,192,384]{2,1,0:T(8,128)(2,1)S(1)}, bf16[3,192,384]{2,1,0:T(8,128)(2,1)}, u32[]{:S(2)}, u32[]{:S(2)}) collective-permute-start(bf16[3,192,384]{2,1,0:T(8,128)(2,1)S(1)} %collective-permute-done.7.refs_13_.refs_14_), channel_id=1, source_target_pairs={{0,32},{4,36},{8,40},{12,44},{16,48},{20,52},{24,56},{28,60},{32,0... | collective-permute-start | bytes 1327112 | tf_op jit(solution)/shard_map/ppermute | solution.py:221
  57.0 5.3 %collective-permute-done.10.refs_16_.refs_17_ = bf16[3,192,384]{2,1,0:T(8,128)(2,1)} collective-permute-done((bf16[3,192,384]{2,1,0:T(8,128)(2,1)S(1)}, bf16[3,192,384]{2,1,0:T(8,128)(2,1)}, u32[]{:S(2)}, u32[]{:S(2)}) %collective-permute-start.10) | collective-permute-done | bytes 442400 | tf_op jit(solution)/shard_map/ppermute | solution.py:221
  69.1 17.3 %collective-permute-done.22.refs_7_ = bf16[4,48,1536]{2,1,0:T(8,128)(2,1)} collective-permute-done((bf16[4,48,1536]{2,1,0:T(8,128)(2,1)S(1)}, bf16[4,48,1536]{2,1,0:T(8,128)(2,1)}, u32[]{:S(2)}, u32[]{:S(2)}) %collective-permute-start.22) | collective-permute-done | bytes 589856 | tf_op jit(solution)/shard_map/ppermute | solution.py:221
  95.5 12.6 %shard_map.55 = (bf16[240,384]{1,0:T(8,128)(2,1)S(1)}, bf16[240,384]{1,0:T(8,128)(2,1)S(1)}, bf16[240,384]{1,0:T(8,128)(2,1)S(1)}, bf16[240,384]{1,0:T(8,128)(2,1)S(1)}, bf16[240,1536]{1,0:T(8,128)(2,1)S(1)}) custom-call(s32[4]{0:T(128)S(1)} %pad_add_fusion.refs_0_.meta_ref, bf16[480,384]{1,0:T(8,128)(2,1)S(1)} %copy-done.13, ...), custom_call_target="tpu_custom_call" | custom-call | tf_op jit(solution)/shard_map/pallas_call | solution.py:158
  108.2 3.2 %collective-permute-start.16 = (bf16[240,384]{1,0:T(8,128)(2,1)S(1)}, bf16[240,384]{1,0:T(8,128)(2,1)S(1)}, u32[]{:S(2)}, u32[]{:S(2)}) collective-permute-start(bf16[240,384]{1,0:T(8,128)(2,1)S(1)} %get-tuple-element.24), channel_id=1, source_target_pairs={{0,3},{1,0},{2,1},{3,2},{4,7},{5,4},{6,5},{7,6},{8,11},{9,8},{10,9... | collective-permute-start | bytes 552968 | tf_op jit(solution)/shard_map/ppermute | solution.py:32
  111.6 5.3 %collective-permute-done.15.refs_1_ = bf16[240,384]{1,0:T(8,128)(2,1)S(1)} collective-permute-done((bf16[240,384]{1,0:T(8,128)(2,1)S(1)}, bf16[240,384]{1,0:T(8,128)(2,1)S(1)}, u32[]{:S(2)}, u32[]{:S(2)}) %collective-permute-start.15) | collective-permute-done | bytes 184352 | tf_op jit(solution)/shard_map/ppermute | solution.py:32
  122.7 4.1 %shard_map.56 = (bf16[120,1536]{1,0:T(8,128)(2,1)}, bf16[120,1536]{1,0:T(8,128)(2,1)}) custom-call(s32[4]{0:T(128)S(1)} %pad_add_fusion.refs_0_.meta_ref, bf16[240,384]{1,0:T(8,128)(2,1)S(1)} %get-tuple-element.22.refs_0_, bf16[240,384]{1,0:T(8,128)(2,1)S(1)} %collective-permute-done.15.refs_1_, bf16[240,384]{1,0:T(8,128)(2,1)S(1)} %collective-permute-done.16.refs_2_, ...), custom_call_target="tpu_custom_call" | custom-call | tf_op jit(solution)/shard_map/pallas_call | solution.py:194
  130.8 9.8 %collective-permute-done.43.refs_7_ = bf16[4,48,1536]{2,1,0:T(8,128)(2,1)S(1)} collective-permute-done((bf16[4,48,1536]{2,1,0:T(8,128)(2,1)S(1)}, bf16[4,48,1536]{2,1,0:T(8,128)(2,1)S(1)}, u32[]{:S(2)}, u32[]{:S(2)}) %collective-permute-start.43) | collective-permute-done | bytes 589856 | tf_op jit(solution)/shard_map/ppermute | solution.py:221
  144.8 5.1 %collective-permute-done.30 = bf16[120,1536]{1,0:T(8,128)(2,1)} collective-permute-done((bf16[120,1536]{1,0:T(8,128)(2,1)}, bf16[120,1536]{1,0:T(8,128)(2,1)}, u32[]{:S(2)}, u32[]{:S(2)}) %collective-permute-start.30) | collective-permute-done | bytes 368672 | tf_op jit(solution)/shard_map/ppermute | solution.py:336
  157.4 7.2 %collective-permute-done.32.refs_4_ = bf16[120,1536]{1,0:T(8,128)(2,1)S(1)} collective-permute-done((bf16[120,1536]{1,0:T(8,128)(2,1)}, bf16[120,1536]{1,0:T(8,128)(2,1)S(1)}, u32[]{:S(2)}, u32[]{:S(2)}) %collective-permute-start.32) | collective-permute-done | bytes 368672 | tf_op jit(solution)/shard_map/ppermute | solution.py:331
  165.1 5.1 %collective-permute-done.35.refs_7_ = bf16[120,1536]{1,0:T(8,128)(2,1)S(1)} collective-permute-done((bf16[120,1536]{1,0:T(8,128)(2,1)}, bf16[120,1536]{1,0:T(8,128)(2,1)S(1)}, u32[]{:S(2)}, u32[]{:S(2)}) %collective-permute-start.35) | collective-permute-done | bytes 368672 | tf_op jit(solution)/shard_map/ppermute | solution.py:32
  172.8 7.3 %collective-permute-done.36.refs_8_ = bf16[120,1536]{1,0:T(8,128)(2,1)S(1)} collective-permute-done((bf16[120,1536]{1,0:T(8,128)(2,1)}, bf16[120,1536]{1,0:T(8,128)(2,1)S(1)}, u32[]{:S(2)}, u32[]{:S(2)}) %collective-permute-start.36) | collective-permute-done | bytes 368672 | tf_op jit(solution)/shard_map/ppermute | solution.py:32
  180.1 11.8 %shard_map.57 = (bf16[240,384]{1,0:T(8,128)(2,1)S(1)}, bf16[240,384]{1,0:T(8,128)(2,1)S(1)}, bf16[240,384]{1,0:T(8,128)(2,1)S(1)}, bf16[240,384]{1,0:T(8,128)(2,...) custom-call(s32[4]{0:T(128)S(1)} %pad_add_fusion.refs_0_.meta_ref, ...), custom_call_target="tpu_custom_call" | custom-call | tf_op jit(solution)/shard_map/pallas_call | solution.py:158
  192.0 3.7 %collective-permute-start.41 = (bf16[240,384]{1,0:T(8,128)(2,1)S(1)}, bf16[240,384]{1,0:T(8,128)(2,1)S(1)}, u32[]{:S(2)}, u32[]{:S(2)}) collective-permute-start(bf16[240,384]{1,0:T(8,128)(2,1)S(1)} %get-tuple-element.33), channel_id=1, source_target_pairs={{0,3},{1,0},{2,1},{3,2},{4,7},{5,4},{6,5},{7,6},{8,11},{9,8},{10,9... | collective-permute-start | bytes 552968 | tf_op jit(solution)/shard_map/ppermute | solution.py:32
  215.4 9.9 %collective-permute-done.50.refs_4_ = bf16[240,384]{1,0:T(8,128)(2,1)S(1)} collective-permute-done((bf16[240,384]{1,0:T(8,128)(2,1)S(1)}, bf16[240,384]{1,0:T(8,128)(2,1)S(1)}, u32[]{:S(2)}, u32[]{:S(2)}) %collective-permute-start.50) | collective-permute-done | bytes 184352 | tf_op jit(solution)/shard_map/ppermute | solution.py:286
  230.8 9.9 %collective-permute-done.38.refs_2_ = bf16[2,240,384]{2,1,0:T(8,128)(2,1)S(1)} collective-permute-done((bf16[2,240,384]{2,1,0:T(8,128)(2,1)S(1)}, bf16[2,240,384]{2,1,0:T(8,128)(2,1)S(1)}, u32[]{:S(2)}, u32[]{:S(2)}) %collective-permute-start.38) | collective-permute-done | bytes 368672 | tf_op jit(solution)/shard_map/ppermute | solution.py:347
  240.6 9.4 %collective-permute-done.39.refs_3_ = bf16[2,240,384]{2,1,0:T(8,128)(2,1)S(1)} collective-permute-done((bf16[2,240,384]{2,1,0:T(8,128)(2,1)S(1)}, bf16[2,240,384]{2,1,0:T(8,128)(2,1)S(1)}, u32[]{:S(2)}, u32[]{:S(2)}) %collective-permute-start.39) | collective-permute-done | bytes 368672 | tf_op jit(solution)/shard_map/ppermute | solution.py:346
  250.8 3.4 %finish.1 = bf16[2,30,30,384]{3,2,1,0:T(8,128)(2,1)} custom-call(s32[4]{0:T(128)} %copy-done.29, bf16[2,240,384]{2,1,0:T(8,128)(2,1)} %copy-done.34, bf16[2,240,384]{2,1,0:T(8,128)(2,1)} %copy-done.26, bf16[2,240,384]{2,1,0:T(8,128)(2,1)} %copy-done.35, bf16[2,240,384]{2,1,0:T(8,128)(2,1)} %copy-done.36, bf16[240,384]{1,0:T(8,128)(2,1)} %copy-done.37, ...), custom_call_target="tpu_custom_call" | custom-call | tf_op jit(solution)/shard_map/finish/pallas_call | solution.py:271
  254.2 3.9 %copy.9 = bf16[1,2,30,30,384]{4,1,3,2,0:T(2,128)(2,1)} copy(bf16[1,2,30,30,384]{4,3,2,1,0:T(8,128)(2,1)} %bitcast.26) | data formatting | bytes 2764800 | tf_op jit(solution)/shard_map/broadcast_in_dim | solution.py:350
  (215 shorter events, 92.3 us)
Async XLA Ops:
  16.0 18.1 %collective-permute-start.1 = (bf16[480,384]{1,0:T(8,128)(2,1)S(1)}, bf16[480,384]{1,0:T(8,128)(2,1)S(1)}, u32[]{:S(2)}, u32[]{:S(2)}) collective-permute-start(bf16[480,384]{1,0:T(8,128)(2,1)S(1)} %fusion.5.refs_2_), channel_id=1, source_target_pairs={{0,1},{1,2},{2,3},{3,0},{4,5},{5,6},{6,7},{7,4},{8,9},{9,10},{10,1... | collective-permute-start | bytes 1105928 | tf_op jit(solution)/shard_map/ppermute | solution.py:32
  16.9 17.1 %collective-permute-start = (bf16[480,384]{1,0:T(8,128)(2,1)S(1)}, bf16[480,384]{1,0:T(8,128)(2,1)S(1)}, u32[]{:S(2)}, u32[]{:S(2)}) collective-permute-start(bf16[480,384]{1,0:T(8,128)(2,1)S(1)} %fusion.3.refs_1_), channel_id=1, source_target_pairs={{0,1},{1,2},{2,3},{3,0},{4,5},{5,6},{6,7},{7,4},{8,9},{9,10},{10,1... | collective-permute-start | bytes 1105928 | tf_op jit(solution)/shard_map/ppermute | solution.py:32
  22.8 30.7 %collective-permute-start.21 = (bf16[4,48,1536]{2,1,0:T(8,128)(2,1)}, bf16[4,48,1536]{2,1,0:T(8,128)(2,1)}, u32[]{:S(2)}, u32[]{:S(2)}) collective-permute-start(bf16[4,48,1536]{2,1,0:T(8,128)(2,1)} %pad_maximum_fusion), channel_id=1, source_target_pairs={{0,64},{64,0},{1,65},{65,1},{2,66},{66,2},{3,67},{67,3},{4,68},{68... | collective-permute-start | bytes 1769480 | tf_op jit(solution)/shard_map/ppermute | solution.py:313
  24.9 28.6 %collective-permute-start.8 = (bf16[3,192,384]{2,1,0:T(8,128)(2,1)S(1)}, bf16[3,192,384]{2,1,0:T(8,128)(2,1)S(1)}, u32[]{:S(2)}, u32[]{:S(2)}) collective-permute-start(bf16[3,192,384]{2,1,0:T(8,128)(2,1)S(1)} %collective-permute-done.7.refs_13_.refs_14_), channel_id=1, source_target_pairs={{0,16},{4,20},{8,24},{12,28},{16,32},{20,36},{24,40},{28,44},{32,4... | collective-permute-start | bytes 1327112 | tf_op jit(solution)/shard_map/ppermute | solution.py:221
  26.5 27.4 %collective-permute-start.9 = (bf16[3,192,384]{2,1,0:T(8,128)(2,1)S(1)}, bf16[3,192,384]{2,1,0:T(8,128)(2,1)}, u32[]{:S(2)}, u32[]{:S(2)}) collective-permute-start(bf16[3,192,384]{2,1,0:T(8,128)(2,1)S(1)} %collective-permute-done.7.refs_13_.refs_14_), channel_id=1, source_target_pairs={{0,48},{4,52},{8,56},{12,60},{16,0},{20,4},{24,8},{28,12},{32,16},... | collective-permute-start | bytes 1327112 | tf_op jit(solution)/shard_map/ppermute | solution.py:221
  56.3 30.1 %collective-permute-start.22 = (bf16[4,48,1536]{2,1,0:T(8,128)(2,1)S(1)}, bf16[4,48,1536]{2,1,0:T(8,128)(2,1)}, u32[]{:S(2)}, u32[]{:S(2)}) collective-permute-start(bf16[4,48,1536]{2,1,0:T(8,128)(2,1)S(1)} %get-tuple-element.40.refs_6_), channel_id=1, source_target_pairs={{0,16},{4,20},{8,24},{12,28},{16,32},{20,36},{24,40},{28,44},{32,4... | collective-permute-start | bytes 1769480 | tf_op jit(solution)/shard_map/ppermute | solution.py:221
  62.2 45.9 %collective-permute-start.23 = (bf16[4,48,1536]{2,1,0:T(8,128)(2,1)S(1)}, bf16[4,48,1536]{2,1,0:T(8,128)(2,1)}, u32[]{:S(2)}, u32[]{:S(2)}) collective-permute-start(bf16[4,48,1536]{2,1,0:T(8,128)(2,1)S(1)} %get-tuple-element.40.refs_6_), channel_id=1, source_target_pairs={{0,48},{4,52},{8,56},{12,60},{16,0},{20,4},{24,8},{28,12},{32,16},... | collective-permute-start | bytes 1769480 | tf_op jit(solution)/shard_map/ppermute | solution.py:221
  65.8 45.6 %collective-permute-start.24 = (bf16[4,48,1536]{2,1,0:T(8,128)(2,1)S(1)}, bf16[4,48,1536]{2,1,0:T(8,128)(2,1)}, u32[]{:S(2)}, u32[]{:S(2)}) collective-permute-start(bf16[4,48,1536]{2,1,0:T(8,128)(2,1)S(1)} %get-tuple-element.40.refs_6_), channel_id=1, source_target_pairs={{0,32},{4,36},{8,40},{12,44},{16,48},{20,52},{24,56},{28,60},{32,0... | collective-permute-start | bytes 1769480 | tf_op jit(solution)/shard_map/ppermute | solution.py:221
  67.9 18.7 %collective-permute-start.14 = (bf16[3,192,384]{2,1,0:T(8,128)(2,1)}, bf16[3,192,384]{2,1,0:T(8,128)(2,1)}, u32[]{:S(2)}, u32[]{:S(2)}) collective-permute-start(bf16[3,192,384]{2,1,0:T(8,128)(2,1)} %collective-permute-done.10.refs_16_.refs_17_), channel_id=1, source_target_pairs={{0,4},{4,0},{8,12},{12,8},{16,20},{20,16},{24,28},{28,24},{32,36},... | collective-permute-start | bytes 1327112 | tf_op jit(solution)/shard_map/ppermute | solution.py:230
  68.6 42.9 %collective-permute-start.25 = (bf16[4,48,1536]{2,1,0:T(8,128)(2,1)S(1)}, bf16[4,48,1536]{2,1,0:T(8,128)(2,1)}, u32[]{:S(2)}, u32[]{:S(2)}) collective-permute-start(bf16[4,48,1536]{2,1,0:T(8,128)(2,1)S(1)} %get-tuple-element.40.refs_6_), channel_id=1, source_target_pairs={{0,4},{4,0},{8,12},{12,8},{16,20},{20,16},{24,28},{28,24},{32,36},... | collective-permute-start | bytes 1769480 | tf_op jit(solution)/shard_map/ppermute | solution.py:230
  86.4 34.0 %collective-permute-start.26 = (bf16[4,48,1536]{2,1,0:T(8,128)(2,1)}, bf16[4,48,1536]{2,1,0:T(8,128)(2,1)S(1)}, u32[]{:S(2)}, u32[]{:S(2)}) collective-permute-start(bf16[4,48,1536]{2,1,0:T(8,128)(2,1)} %collective-permute-done.22.refs_7_), channel_id=1, source_target_pairs={{0,4},{4,0},{8,12},{12,8},{16,20},{20,16},{24,28},{28,24},{32,36},... | collective-permute-start | bytes 1769480 | tf_op jit(solution)/shard_map/ppermute | solution.py:230
  111.5 29.1 %collective-permute-start.43 = (bf16[4,48,1536]{2,1,0:T(8,128)(2,1)S(1)}, bf16[4,48,1536]{2,1,0:T(8,128)(2,1)S(1)}, u32[]{:S(2)}, u32[]{:S(2)}) collective-permute-start(bf16[4,48,1536]{2,1,0:T(8,128)(2,1)S(1)} %get-tuple-element.39.refs_6_), channel_id=1, source_target_pairs={{0,16},{4,20},{8,24},{12,28},{16,32},{20,36},{24,40},{28,44},{32,4... | collective-permute-start | bytes 1769480 | tf_op jit(solution)/shard_map/ppermute | solution.py:221
  116.9 23.7 %collective-permute-start.44 = (bf16[4,48,1536]{2,1,0:T(8,128)(2,1)S(1)}, bf16[4,48,1536]{2,1,0:T(8,128)(2,1)S(1)}, u32[]{:S(2)}, u32[]{:S(2)}) collective-permute-start(bf16[4,48,1536]{2,1,0:T(8,128)(2,1)S(1)} %get-tuple-element.39.refs_6_), channel_id=1, source_target_pairs={{0,48},{4,52},{8,56},{12,60},{16,0},{20,4},{24,8},{28,12},{32,16},... | collective-permute-start | bytes 1769480 | tf_op jit(solution)/shard_map/ppermute | solution.py:221
  120.5 23.8 %collective-permute-start.45 = (bf16[4,48,1536]{2,1,0:T(8,128)(2,1)S(1)}, bf16[4,48,1536]{2,1,0:T(8,128)(2,1)}, u32[]{:S(2)}, u32[]{:S(2)}) collective-permute-start(bf16[4,48,1536]{2,1,0:T(8,128)(2,1)S(1)} %get-tuple-element.39.refs_6_), channel_id=1, source_target_pairs={{0,32},{4,36},{8,40},{12,44},{16,48},{20,52},{24,56},{28,60},{32,0... | collective-permute-start | bytes 1769480 | tf_op jit(solution)/shard_map/ppermute | solution.py:221
  126.8 23.1 %collective-permute-start.30 = (bf16[120,1536]{1,0:T(8,128)(2,1)}, bf16[120,1536]{1,0:T(8,128)(2,1)}, u32[]{:S(2)}, u32[]{:S(2)}) collective-permute-start(bf16[120,1536]{1,0:T(8,128)(2,1)} %get-tuple-element.28), channel_id=1, source_target_pairs={{4,0},{5,1},{8,4},{9,5},{12,8},{13,9},{16,12},{17,13},{20,16},{21,... | collective-permute-start | bytes 1105928 | tf_op jit(solution)/shard_map/ppermute | solution.py:336
  128.7 25.6 %collective-permute-start.34 = (bf16[120,1536]{1,0:T(8,128)(2,1)}, bf16[120,1536]{1,0:T(8,128)(2,1)}, u32[]{:S(2)}, u32[]{:S(2)}) collective-permute-start(bf16[120,1536]{1,0:T(8,128)(2,1)} %get-tuple-element.28), channel_id=1, source_target_pairs={{4,3},{5,0},{2,1},{3,2},{8,7},{9,4},{6,5},{7,6},{12,11},{13,8},{10... | collective-permute-start | bytes 1105928 | tf_op jit(solution)/shard_map/ppermute | solution.py:331
  144.3 47.8 %collective-permute-start.46 = (bf16[4,48,1536]{2,1,0:T(8,128)(2,1)S(1)}, bf16[4,48,1536]{2,1,0:T(8,128)(2,1)S(1)}, u32[]{:S(2)}, u32[]{:S(2)}) collective-permute-start(bf16[4,48,1536]{2,1,0:T(8,128)(2,1)S(1)} %get-tuple-element.39.refs_6_), channel_id=1, source_target_pairs={{0,4},{4,0},{8,12},{12,8},{16,20},{20,16},{24,28},{28,24},{32,36},... | collective-permute-start | bytes 1769480 | tf_op jit(solution)/shard_map/ppermute | solution.py:230
  149.9 45.8 %collective-permute-start.47 = (bf16[4,48,1536]{2,1,0:T(8,128)(2,1)}, bf16[4,48,1536]{2,1,0:T(8,128)(2,1)S(1)}, u32[]{:S(2)}, u32[]{:S(2)}) collective-permute-start(bf16[4,48,1536]{2,1,0:T(8,128)(2,1)} %copy-done.14), channel_id=1, source_target_pairs={{0,4},{4,0},{8,12},{12,8},{16,20},{20,16},{24,28},{28,24},{32,36},... | collective-permute-start | bytes 1769480 | tf_op jit(solution)/shard_map/ppermute | solution.py:230
  164.6 32.6 %collective-permute-start.48 = (bf16[4,48,1536]{2,1,0:T(8,128)(2,1)}, bf16[4,48,1536]{2,1,0:T(8,128)(2,1)S(1)}, u32[]{:S(2)}, u32[]{:S(2)}) collective-permute-start(bf16[4,48,1536]{2,1,0:T(8,128)(2,1)} %copy-done.16), channel_id=1, source_target_pairs={{0,4},{4,0},{8,12},{12,8},{16,20},{20,16},{24,28},{28,24},{32,36},... | collective-permute-start | bytes 1769480 | tf_op jit(solution)/shard_map/ppermute | solution.py:230
  165.1 32.1 %collective-permute-start.49 = (bf16[4,48,1536]{2,1,0:T(8,128)(2,1)}, bf16[4,48,1536]{2,1,0:T(8,128)(2,1)S(1)}, u32[]{:S(2)}, u32[]{:S(2)}) collective-permute-start(bf16[4,48,1536]{2,1,0:T(8,128)(2,1)} %collective-permute-done.45.refs_9_), channel_id=1, source_target_pairs={{0,4},{4,0},{8,12},{12,8},{16,20},{20,16},{24,28},{28,24},{32,36},... | collective-permute-start | bytes 1769480 | tf_op jit(solution)/shard_map/ppermute | solution.py:230
  207.6 17.7 %collective-permute-start.50 = (bf16[240,384]{1,0:T(8,128)(2,1)S(1)}, bf16[240,384]{1,0:T(8,128)(2,1)S(1)}, u32[]{:S(2)}, u32[]{:S(2)}) collective-permute-start(bf16[240,384]{1,0:T(8,128)(2,1)S(1)} %get-tuple-element.35.refs_8_), channel_id=1, source_target_pairs={{0,64},{1,65},{2,66},{3,67},{4,68},{5,69},{6,70},{7,71},{8,72},{9,... | collective-permute-start | bytes 552968 | tf_op jit(solution)/shard_map/ppermute | solution.py:286
  208.9 17.1 %collective-permute-start.51 = (bf16[240,384]{1,0:T(8,128)(2,1)S(1)}, bf16[240,384]{1,0:T(8,128)(2,1)}, u32[]{:S(2)}, u32[]{:S(2)}) collective-permute-start(bf16[240,384]{1,0:T(8,128)(2,1)S(1)} %get-tuple-element.36), channel_id=1, source_target_pairs={{0,65},{1,66},{2,67},{3,64},{4,69},{5,70},{6,71},{7,68},{8,73},{9,... | collective-permute-start | bytes 552968 | tf_op jit(solution)/shard_map/ppermute | solution.py:286
  212.2 18.6 %collective-permute-start.37 = (bf16[2,240,384]{2,1,0:T(8,128)(2,1)S(1)}, bf16[2,240,384]{2,1,0:T(8,128)(2,1)S(1)}, u32[]{:S(2)}, u32[]{:S(2)}) collective-permute-start(bf16[2,240,384]{2,1,0:T(8,128)(2,1)S(1)} %get-tuple-element.29), channel_id=1, source_target_pairs={{0,4},{4,8},{8,12},{12,16},{16,20},{20,24},{24,28},{28,32},{32,36}... | collective-permute-start | bytes 1105928 | tf_op jit(solution)/shard_map/ppermute | solution.py:345
  228.0 22.0 %collective-permute-start.39 = (bf16[2,240,384]{2,1,0:T(8,128)(2,1)S(1)}, bf16[2,240,384]{2,1,0:T(8,128)(2,1)S(1)}, u32[]{:S(2)}, u32[]{:S(2)}) collective-permute-start(bf16[2,240,384]{2,1,0:T(8,128)(2,1)S(1)} %get-tuple-element.30.refs_1_), channel_id=1, source_target_pairs={{64,0},{65,1},{66,2},{67,3},{68,4},{69,5},{70,6},{71,7},{72,8},{73... | collective-permute-start | bytes 1105928 | tf_op jit(solution)/shard_map/ppermute | solution.py:346
  (77 other events, 996.9 us)
